TPU v7x, 256 devices: a whole 4x4x8 slice. The times are simulated.
256 devices in a mesh: slab: 32 (over x, y, core), orb: 8 (over z).
Axes of the slice: x: 4, y: 4, z: 8, core: 2. Of those that a mesh axis runs over, the one named last changes fastest.
Arguments:
- orbitals: float32 [256, 65536], P('orb', 'slab'), may hold values from -6 to 6
- cell_matrices: bfloat16 [256, 512, 512], P('slab'), as said below
- connectivity: int32 [256, 512], P('slab'), may hold values from 0 to 2559, as said below
- face_lower: int32 [8192], P('slab'), may hold values from 0 to 2047, as said below
- face_upper: int32 [8192], P('slab'), may hold values from 0 to 2047, as said below
Outputs:
- orthonormal_orbitals: float32 [256, 65536], P('orb', 'slab')
Inputs may be any that keep to these rules, and one draw needn't show every extreme that they name: `connectivity`: each row names 512 distinct positions of its slab's extended numbering. `face_lower`: each slab's block of 256 entries names distinct own nodes; it shares no entry with the same slab's block of face_upper. `face_upper`: each slab's block of 256 entries names distinct own nodes; it shares no entry with the same slab's block of face_lower. `cell_matrices`: each cell matrix is symmetric.
All inputs are finite; a program needn't handle non-finite values.
Results may differ from a plain program's by a relative error of at most 0.023.
Values may be sent and summed in bfloat16 or wider, within the bound.
A program may use at most 64 MiB of HBM per device.

v0:
```python
import math

import jax
import jax.numpy as jnp
from jax import lax
from jax.sharding import PartitionSpec as P

CELL_NODES = 512
DEGREE = 4
FACE = 256


def extended_2(cells, sides, width):
    for axis, dim in sides:
        count = lax.axis_size(axis)
        ends = count - 1
        head = lax.slice_in_dim(cells, 0, width, axis=dim)
        tail = lax.slice_in_dim(cells, cells.shape[dim] - width, cells.shape[dim], axis=dim)
        cells = jnp.concatenate(
            [
                lax.ppermute(tail, axis, [(i, (i + 1) % count) for i in range(ends)]),
                cells,
                lax.ppermute(head, axis, [((i + 1) % count, i) for i in range(ends)]),
            ],
            axis=dim,
        )
    return cells


def partner_2(value, axis, distance):
    mask = 2**distance
    pairs = [(source, source ^ mask) for source in range(lax.axis_size(axis))]
    return lax.ppermute(value, axis, pairs)


def gram_of(matrix):
    return lax.dot_general(
        matrix,
        matrix,
        (((1,), (1,)), ((), ())),
        precision=lax.Precision.HIGHEST,
        preferred_element_type=jnp.float32,
    )


def forward_solve(factor, values):
    return lax.linalg.triangular_solve(factor, values, left_side=True, lower=True)


def three_parts(values):
    upper_part = values.astype(jnp.bfloat16)
    remain = values - upper_part.astype(jnp.float32)
    middle_part = remain.astype(jnp.bfloat16)
    lowest_part = (remain - middle_part.astype(jnp.float32)).astype(jnp.bfloat16)
    return jnp.concatenate([upper_part, middle_part, lowest_part], axis=0)


def spread_back(values, table):
    row_count = values.shape[0]
    stacked = lax.dot_general(
        three_parts(values), table, (((1,), (1,)), ((), ())), preferred_element_type=jnp.float32
    )
    return stacked[:row_count] + stacked[row_count : 2 * row_count] + stacked[2 * row_count :]


def apply_cells(wave_field, cell_matrices, connectivity, face_table):
    rounded = wave_field.astype(jnp.bfloat16)
    orb_count, node_count = rounded.shape
    face_rows = jnp.dot(rounded, face_table, preferred_element_type=jnp.float32).astype(
        jnp.bfloat16
    )
    bordered = extended_2(face_rows, (("slab", 1),), FACE)
    extended = jnp.concatenate([bordered[:, :FACE], rounded, bordered[:, 3 * FACE :]], axis=1)
    ext_count = extended.shape[1]
    positions = lax.broadcasted_iota(jnp.int32, (ext_count, CELL_NODES), 0)

    def add_cell(summed, inputs):
        cell_block, cell_row = inputs
        picker = (positions == cell_row[None, :]).astype(jnp.bfloat16)
        pieces = jnp.dot(extended, picker, preferred_element_type=jnp.float32).astype(jnp.bfloat16)
        cell_terms = jnp.dot(pieces, cell_block, preferred_element_type=jnp.float32)
        return (summed + spread_back(cell_terms, picker), None)

    summed, _ = lax.scan(
        add_cell, jnp.zeros((orb_count, ext_count), jnp.float32), (cell_matrices, connectivity)
    )
    returned = jnp.concatenate([summed[:, :FACE], summed[:, FACE + node_count :]], axis=1)
    received = extended_2(returned, (("slab", 1),), FACE)
    incoming = jnp.concatenate([received[:, :FACE], received[:, 3 * FACE :]], axis=1)
    return summed[:, FACE : FACE + node_count] + spread_back(incoming, face_table)


def per_device(orbitals, cell_matrices, connectivity, face_lower, face_upper):
    node_count = orbitals.shape[1]
    face_nodes = jnp.concatenate([face_lower, face_upper], axis=0)
    face_table = (
        lax.broadcasted_iota(jnp.int32, (node_count, face_nodes.shape[0]), 0) == face_nodes[None, :]
    ).astype(jnp.bfloat16)
    previous = orbitals
    current = apply_cells(orbitals, cell_matrices, connectivity, face_table)
    for degree_step in range(1, DEGREE):
        following = 2.0 * apply_cells(current, cell_matrices, connectivity, face_table) - previous
        previous, current = (current, following)
    block_rows = orbitals.shape[0]
    norm_scale = math.sqrt(orbitals.shape[1] * lax.axis_size("slab"))
    gathered = lax.all_gather(current.astype(jnp.bfloat16), "orb", axis=0, tiled=True).astype(
        current.dtype
    )
    factor = jnp.linalg.cholesky(gram_of(gathered))
    for level in range(lax.axis_size("slab").bit_length() - 1):
        partner = partner_2(factor.astype(jnp.bfloat16), "slab", level).astype(factor.dtype)
        factor = jnp.linalg.cholesky(gram_of(factor) + gram_of(partner))
    solved = forward_solve(factor, gathered) * norm_scale
    result = lax.dynamic_slice_in_dim(solved, lax.axis_index("orb") * block_rows, block_rows, 0)
    return result


def solution(mesh):
    in_specs = (P("orb", "slab"), P("slab", None, None), P("slab", None), P("slab"), P("slab"))
    out_specs = P("orb", "slab")
    return jax.shard_map(
        per_device, mesh=mesh, in_specs=in_specs, out_specs=out_specs, check_vma=False
    )
```

profile of v0, /device:TPU:2, one launch (start us, length us, event | category | flops | bytes accessed | tf_op | source)
XLA Modules:
  0.0 538.3 jit_solution(7230007769574144148)
XLA Ops:
  10.9 5.8 %collective-permute-start.1 = (bf16[32,256]{1,0:T(8,128)(2,1)S(1)}, bf16[32,256]{1,0:T(8,128)(2,1)S(1)}, u32[]{:S(2)}, u32[]{:S(2)}) collective-permute-start(bf16[32,256]{1,0:T(8,128)(2,1)S(1)} %get-tuple-element.343), channel_id=1, source_target_pairs={{8,0},{16,8},{24,16},{32,24},{40,32},{48,40},{56,48},{64,56},{72,6... | collective-permute-start | bytes 49160 | tf_op jit(solution)/shard_map/ppermute | solution.py:23
  18.1 33.1 %while.46 = (s32[]{:T(128)}, f32[32,2560]{1,0:T(8,128)S(1)}, s32[8,512]{1,0:T(8,128)}, bf16[32,2560]{1,0:T(8,128)(2,1)S(1)}, bf16[8,512,512]{2,1,0:T(8,128)(2,1)}, /*index=5*/s32[]{:T(128)}, s32[]{:T(128)}) while((s32[]{:T(128)}, f32[32,2560]{1,0:T(8,128)S(1)}, s32[8,512]{1,0:T(8,128)}, bf16[32,2560]{1,0:T(8,128)(2,1)S(1)}, ...), condition=%wide.region_1.2_spmd.clone, body=%wide.region_0.1_spmd.clone.sunk | while | flops 357007360 | bytes 3514971 | solution.py:84
  53.2 5.8 %collective-permute-start.3 = (f32[32,256]{1,0:T(8,128)S(1)}, f32[32,256]{1,0:T(8,128)S(1)}, u32[]{:S(2)}, u32[]{:S(2)}) collective-permute-start(f32[32,256]{1,0:T(8,128)S(1)} %get-tuple-element.298), channel_id=1, source_target_pairs={{8,0},{16,8},{24,16},{32,24},{40,32},{48,40},{56,48},{64,56},{72,6... | collective-permute-start | bytes 98312 | tf_op jit(solution)/shard_map/ppermute | solution.py:23
  64.3 5.8 %collective-permute-start.5 = (bf16[32,256]{1,0:T(8,128)(2,1)S(1)}, bf16[32,256]{1,0:T(8,128)(2,1)S(1)}, u32[]{:S(2)}, u32[]{:S(2)}) collective-permute-start(bf16[32,256]{1,0:T(8,128)(2,1)S(1)} %get-tuple-element.341), channel_id=1, source_target_pairs={{8,0},{16,8},{24,16},{32,24},{40,32},{48,40},{56,48},{64,56},{72,6... | collective-permute-start | bytes 49160 | tf_op jit(solution)/shard_map/ppermute | solution.py:23
  71.5 27.5 %while.47 = (s32[]{:T(128)}, f32[32,2560]{1,0:T(8,128)S(1)}, s32[8,512]{1,0:T(8,128)S(1)}, bf16[32,2560]{1,0:T(8,128)(2,1)S(1)}, bf16[8,512,512]{2,1,0:T(8,128)(2,1)}, /*index=5*/s32[]{:T(128)}, s32[]{:T(128)}) while((s32[]{:T(128)}, f32[32,2560]{1,0:T(8,128)S(1)}, s32[8,512]{1,0:T(8,128)S(1)}, bf16[32,2560]{1,0:T(8,128)(2,1)S(1)}, ...), condition=%wide.region_3.4_spmd.clone, body=%wide.region_2.3_spmd.clone.sunk | while | flops 357007360 | bytes 3514971 | solution.py:84
  101.0 5.8 %collective-permute-start.7 = (f32[32,256]{1,0:T(8,128)S(1)}, f32[32,256]{1,0:T(8,128)S(1)}, u32[]{:S(2)}, u32[]{:S(2)}) collective-permute-start(f32[32,256]{1,0:T(8,128)S(1)} %get-tuple-element.296), channel_id=1, source_target_pairs={{8,0},{16,8},{24,16},{32,24},{40,32},{48,40},{56,48},{64,56},{72,6... | collective-permute-start | bytes 98312 | tf_op jit(solution)/shard_map/ppermute | solution.py:23
  112.1 5.8 %collective-permute-start.9 = (bf16[32,256]{1,0:T(8,128)(2,1)S(1)}, bf16[32,256]{1,0:T(8,128)(2,1)S(1)}, u32[]{:S(2)}, u32[]{:S(2)}) collective-permute-start(bf16[32,256]{1,0:T(8,128)(2,1)S(1)} %get-tuple-element.339), channel_id=1, source_target_pairs={{8,0},{16,8},{24,16},{32,24},{40,32},{48,40},{56,48},{64,56},{72,6... | collective-permute-start | bytes 49160 | tf_op jit(solution)/shard_map/ppermute | solution.py:23
  119.3 27.5 %while.48 = (s32[]{:T(128)}, f32[32,2560]{1,0:T(8,128)S(1)}, s32[8,512]{1,0:T(8,128)S(1)}, bf16[32,2560]{1,0:T(8,128)(2,1)S(1)}, bf16[8,512,512]{2,1,0:T(8,128)(2,1)}, /*index=5*/s32[]{:T(128)}, s32[]{:T(128)}) while((s32[]{:T(128)}, f32[32,2560]{1,0:T(8,128)S(1)}, s32[8,512]{1,0:T(8,128)S(1)}, bf16[32,2560]{1,0:T(8,128)(2,1)S(1)}, ...), condition=%wide.region_5.6_spmd.clone, body=%wide.region_4.5_spmd.clone.sunk | while | flops 357007360 | bytes 3514971 | solution.py:84
  148.7 6.0 %collective-permute-start.11 = (f32[32,256]{1,0:T(8,128)S(1)}, f32[32,256]{1,0:T(8,128)S(1)}, u32[]{:S(2)}, u32[]{:S(2)}) collective-permute-start(f32[32,256]{1,0:T(8,128)S(1)} %get-tuple-element.294), channel_id=1, source_target_pairs={{8,0},{16,8},{24,16},{32,24},{40,32},{48,40},{56,48},{64,56},{72,6... | collective-permute-start | bytes 98312 | tf_op jit(solution)/shard_map/ppermute | solution.py:23
  159.8 5.8 %collective-permute-start.13 = (bf16[32,256]{1,0:T(8,128)(2,1)S(1)}, bf16[32,256]{1,0:T(8,128)(2,1)S(1)}, u32[]{:S(2)}, u32[]{:S(2)}) collective-permute-start(bf16[32,256]{1,0:T(8,128)(2,1)S(1)} %get-tuple-element.337), channel_id=1, source_target_pairs={{8,0},{16,8},{24,16},{32,24},{40,32},{48,40},{56,48},{64,56},{72,6... | collective-permute-start | bytes 49160 | tf_op jit(solution)/shard_map/ppermute | solution.py:23
  167.0 27.5 %while.49 = (s32[]{:T(128)}, f32[32,2560]{1,0:T(8,128)S(1)}, s32[8,512]{1,0:T(8,128)S(1)}, bf16[32,2560]{1,0:T(8,128)(2,1)S(1)}, bf16[8,512,512]{2,1,0:T(8,128)(2,1)}, /*index=5*/s32[]{:T(128)}, s32[]{:T(128)}) while((s32[]{:T(128)}, f32[32,2560]{1,0:T(8,128)S(1)}, s32[8,512]{1,0:T(8,128)S(1)}, bf16[32,2560]{1,0:T(8,128)(2,1)S(1)}, ...), condition=%wide.region_7.8_spmd.clone, body=%wide.region_6.7_spmd.clone.sunk | while | flops 357007360 | bytes 3514971 | solution.py:84
  205.5 41.9 %all-gather.2.cloned.1.call-done = bf16[256,2048]{1,0:T(8,128)(2,1)} async-done(((bf16[32,2048]{1,0:T(8,128)(2,1)}), bf16[256,2048]{1,0:T(8,128)(2,1)}) %all-gather.2.cloned.1.call-update) | async-done | bytes 1048592 | tf_op jit(solution)/shard_map/all_gather | solution.py:106
  249.7 11.7 %cholesky.298 = f32[128,128]{1,0:T(8,128)S(1)} custom-call(f32[128,128]{1,0:T(8,128)S(1)} %cholesky.498), custom_call_target="Cholesky" | custom-call | tf_op jit(solution)/shard_map/jit(cholesky)/cholesky | solution.py:109
  261.4 9.8 %custom-call.21 = f32[1,128,128]{1,2,0:T(8,128)S(1)} custom-call(f32[1,128,128]{2,1,0:T(8,128)S(1)} %get-tuple-element.323), custom_call_target="InvertDiagBlocksLowerTriangular" | custom-call | tf_op jit(solution)/shard_map/jit(cholesky)/cholesky | solution.py:109
  271.7 11.7 %cholesky.315 = f32[128,128]{1,0:T(8,128)S(1)} custom-call(f32[128,128]{1,0:T(8,128)S(1)} %convolution_subtract_fusion.1), custom_call_target="Cholesky" | custom-call | tf_op jit(solution)/shard_map/jit(cholesky)/cholesky | solution.py:109
  285.4 8.4 %collective-permute-start.16 = (bf16[256,256]{1,0:T(8,128)(2,1)S(1)}, bf16[256,256]{1,0:T(8,128)(2,1)S(1)}, u32[]{:S(2)}, u32[]{:S(2)}) collective-permute-start(bf16[256,256]{1,0:T(8,128)(2,1)S(1)} %fusion.143), channel_id=1, source_target_pairs={{0,8},{8,0},{16,24},{24,16},{32,40},{40,32},{48,56},{56,48},{64,72... | collective-permute-start | bytes 393224 | tf_op jit(solution)/shard_map/ppermute | solution.py:33
  295.5 11.7 %cholesky.332 = f32[128,128]{1,0:T(8,128)S(1)} custom-call(f32[128,128]{1,0:T(8,128)S(1)} %cholesky.501), custom_call_target="Cholesky" | custom-call | tf_op jit(solution)/shard_map/jit(cholesky)/cholesky | solution.py:112
  307.3 9.8 %custom-call.22 = f32[1,128,128]{1,2,0:T(8,128)S(1)} custom-call(f32[1,128,128]{2,1,0:T(8,128)S(1)} %get-tuple-element.319), custom_call_target="InvertDiagBlocksLowerTriangular" | custom-call | tf_op jit(solution)/shard_map/jit(cholesky)/cholesky | solution.py:112
  317.6 11.7 %cholesky.349 = f32[128,128]{1,0:T(8,128)S(1)} custom-call(f32[128,128]{1,0:T(8,128)S(1)} %slice_subtract_fusion.4), custom_call_target="Cholesky" | custom-call | tf_op jit(solution)/shard_map/jit(cholesky)/cholesky | solution.py:112
  338.1 11.7 %cholesky.366 = f32[128,128]{1,0:T(8,128)S(1)} custom-call(f32[128,128]{1,0:T(8,128)S(1)} %cholesky.504), custom_call_target="Cholesky" | custom-call | tf_op jit(solution)/shard_map/jit(cholesky)/cholesky | solution.py:112
  349.9 9.8 %custom-call.23 = f32[1,128,128]{1,2,0:T(8,128)S(1)} custom-call(f32[1,128,128]{2,1,0:T(8,128)S(1)} %get-tuple-element.315), custom_call_target="InvertDiagBlocksLowerTriangular" | custom-call | tf_op jit(solution)/shard_map/jit(cholesky)/cholesky | solution.py:112
  360.2 11.7 %cholesky.383 = f32[128,128]{1,0:T(8,128)S(1)} custom-call(f32[128,128]{1,0:T(8,128)S(1)} %slice_subtract_fusion.3), custom_call_target="Cholesky" | custom-call | tf_op jit(solution)/shard_map/jit(cholesky)/cholesky | solution.py:112
  381.8 11.7 %cholesky.400 = f32[128,128]{1,0:T(8,128)S(1)} custom-call(f32[128,128]{1,0:T(8,128)S(1)} %cholesky.507), custom_call_target="Cholesky" | custom-call | tf_op jit(solution)/shard_map/jit(cholesky)/cholesky | solution.py:112
  393.6 9.8 %custom-call.24 = f32[1,128,128]{1,2,0:T(8,128)S(1)} custom-call(f32[1,128,128]{2,1,0:T(8,128)S(1)} %get-tuple-element.311), custom_call_target="InvertDiagBlocksLowerTriangular" | custom-call | tf_op jit(solution)/shard_map/jit(cholesky)/cholesky | solution.py:112
  403.9 11.7 %cholesky.417 = f32[128,128]{1,0:T(8,128)S(1)} custom-call(f32[128,128]{1,0:T(8,128)S(1)} %slice_subtract_fusion.2), custom_call_target="Cholesky" | custom-call | tf_op jit(solution)/shard_map/jit(cholesky)/cholesky | solution.py:112
  423.8 11.7 %cholesky.434 = f32[128,128]{1,0:T(8,128)S(1)} custom-call(f32[128,128]{1,0:T(8,128)S(1)} %cholesky.510), custom_call_target="Cholesky" | custom-call | tf_op jit(solution)/shard_map/jit(cholesky)/cholesky | solution.py:112
  435.6 9.8 %custom-call.25 = f32[1,128,128]{1,2,0:T(8,128)S(1)} custom-call(f32[1,128,128]{2,1,0:T(8,128)S(1)} %get-tuple-element.307), custom_call_target="InvertDiagBlocksLowerTriangular" | custom-call | tf_op jit(solution)/shard_map/jit(cholesky)/cholesky | solution.py:112
  445.9 11.7 %cholesky.451 = f32[128,128]{1,0:T(8,128)S(1)} custom-call(f32[128,128]{1,0:T(8,128)S(1)} %slice_subtract_fusion.1), custom_call_target="Cholesky" | custom-call | tf_op jit(solution)/shard_map/jit(cholesky)/cholesky | solution.py:112
  467.4 11.7 %cholesky.468 = f32[128,128]{1,0:T(8,128)S(1)} custom-call(f32[128,128]{1,0:T(8,128)S(1)} %cholesky.513), custom_call_target="Cholesky" | custom-call | tf_op jit(solution)/shard_map/jit(cholesky)/cholesky | solution.py:112
  479.1 9.8 %custom-call.26 = f32[1,128,128]{1,2,0:T(8,128)S(1)} custom-call(f32[1,128,128]{2,1,0:T(8,128)S(1)} %get-tuple-element.303), custom_call_target="InvertDiagBlocksLowerTriangular" | custom-call | tf_op jit(solution)/shard_map/jit(cholesky)/cholesky | solution.py:112
  489.4 11.7 %cholesky.485 = f32[128,128]{1,0:T(8,128)S(1)} custom-call(f32[128,128]{1,0:T(8,128)S(1)} %slice_subtract_fusion), custom_call_target="Cholesky" | custom-call | tf_op jit(solution)/shard_map/jit(cholesky)/cholesky | solution.py:112
  507.8 19.7 %custom-call.11 = f32[2,128,128]{1,2,0:T(8,128)S(1)} custom-call(f32[2,128,128]{2,1,0:T(8,128)S(1)} %get-tuple-element.145), custom_call_target="InvertDiagBlocksLowerTriangular" | custom-call | tf_op jit(solution)/shard_map/triangular_solve | solution.py:47
  (302 shorter events, 208.9 us)
Async XLA Ops:
  6.5 240.9 %all-gather.2.cloned.1.call-start = ((), (), s32[]{:S(2)}) async-start(), calls=%async_computation | async-start | bytes 1179648 | tf_op jit(solution)/shard_map/all_gather | solution.py:106
  9.0 7.7 %collective-permute-start = (bf16[32,256]{1,0:T(8,128)(2,1)S(1)}, bf16[32,256]{1,0:T(8,128)(2,1)S(1)}, u32[]{:S(2)}, u32[]{:S(2)}) collective-permute-start(bf16[32,256]{1,0:T(8,128)(2,1)S(1)} %get-tuple-element.342), channel_id=1, source_target_pairs={{0,8},{8,16},{16,24},{24,32},{32,40},{40,48},{48,56},{56,64},{64,7... | collective-permute-start | bytes 49160 | tf_op jit(solution)/shard_map/ppermute | solution.py:21
  10.9 7.2 %collective-permute-start.1 = (bf16[32,256]{1,0:T(8,128)(2,1)S(1)}, bf16[32,256]{1,0:T(8,128)(2,1)S(1)}, u32[]{:S(2)}, u32[]{:S(2)}) collective-permute-start(bf16[32,256]{1,0:T(8,128)(2,1)S(1)} %get-tuple-element.343), channel_id=1, source_target_pairs={{8,0},{16,8},{24,16},{32,24},{40,32},{48,40},{56,48},{64,56},{72,6... | collective-permute-start | bytes 49160 | tf_op jit(solution)/shard_map/ppermute | solution.py:23
  51.3 20.2 %copy-start.2 = (s32[8,512]{1,0:T(8,128)S(1)}, s32[8,512]{1,0:T(8,128)}, u32[]{:S(2)}) copy-start(s32[8,512]{1,0:T(8,128)} %get-tuple-element.649) | copy-start | bytes 49156
  51.3 7.7 %collective-permute-start.2 = (f32[32,256]{1,0:T(8,128)S(1)}, f32[32,256]{1,0:T(8,128)S(1)}, u32[]{:S(2)}, u32[]{:S(2)}) collective-permute-start(f32[32,256]{1,0:T(8,128)S(1)} %get-tuple-element.299), channel_id=1, source_target_pairs={{0,8},{8,16},{16,24},{24,32},{32,40},{40,48},{48,56},{56,64},{64,7... | collective-permute-start | bytes 98312 | tf_op jit(solution)/shard_map/ppermute | solution.py:21
  53.2 7.3 %collective-permute-start.3 = (f32[32,256]{1,0:T(8,128)S(1)}, f32[32,256]{1,0:T(8,128)S(1)}, u32[]{:S(2)}, u32[]{:S(2)}) collective-permute-start(f32[32,256]{1,0:T(8,128)S(1)} %get-tuple-element.298), channel_id=1, source_target_pairs={{8,0},{16,8},{24,16},{32,24},{40,32},{48,40},{56,48},{64,56},{72,6... | collective-permute-start | bytes 98312 | tf_op jit(solution)/shard_map/ppermute | solution.py:23
  62.3 7.7 %collective-permute-start.4 = (bf16[32,256]{1,0:T(8,128)(2,1)S(1)}, bf16[32,256]{1,0:T(8,128)(2,1)S(1)}, u32[]{:S(2)}, u32[]{:S(2)}) collective-permute-start(bf16[32,256]{1,0:T(8,128)(2,1)S(1)} %get-tuple-element.340), channel_id=1, source_target_pairs={{0,8},{8,16},{16,24},{24,32},{32,40},{40,48},{48,56},{56,64},{64,7... | collective-permute-start | bytes 49160 | tf_op jit(solution)/shard_map/ppermute | solution.py:21
  64.3 7.2 %collective-permute-start.5 = (bf16[32,256]{1,0:T(8,128)(2,1)S(1)}, bf16[32,256]{1,0:T(8,128)(2,1)S(1)}, u32[]{:S(2)}, u32[]{:S(2)}) collective-permute-start(bf16[32,256]{1,0:T(8,128)(2,1)S(1)} %get-tuple-element.341), channel_id=1, source_target_pairs={{8,0},{16,8},{24,16},{32,24},{40,32},{48,40},{56,48},{64,56},{72,6... | collective-permute-start | bytes 49160 | tf_op jit(solution)/shard_map/ppermute | solution.py:23
  71.5 37.7 %copy-start.1 = (f32[32,2048]{1,0:T(8,128)S(1)}, f32[32,2048]{1,0:T(8,128)}, u32[]{:S(2)}) copy-start(f32[32,2048]{1,0:T(8,128)} %param.14) | copy-start | bytes 786436
  99.0 7.7 %collective-permute-start.6 = (f32[32,256]{1,0:T(8,128)S(1)}, f32[32,256]{1,0:T(8,128)S(1)}, u32[]{:S(2)}, u32[]{:S(2)}) collective-permute-start(f32[32,256]{1,0:T(8,128)S(1)} %get-tuple-element.297), channel_id=1, source_target_pairs={{0,8},{8,16},{16,24},{24,32},{32,40},{40,48},{48,56},{56,64},{64,7... | collective-permute-start | bytes 98312 | tf_op jit(solution)/shard_map/ppermute | solution.py:21
  101.0 7.3 %collective-permute-start.7 = (f32[32,256]{1,0:T(8,128)S(1)}, f32[32,256]{1,0:T(8,128)S(1)}, u32[]{:S(2)}, u32[]{:S(2)}) collective-permute-start(f32[32,256]{1,0:T(8,128)S(1)} %get-tuple-element.296), channel_id=1, source_target_pairs={{8,0},{16,8},{24,16},{32,24},{40,32},{48,40},{56,48},{64,56},{72,6... | collective-permute-start | bytes 98312 | tf_op jit(solution)/shard_map/ppermute | solution.py:23
  110.1 7.7 %collective-permute-start.8 = (bf16[32,256]{1,0:T(8,128)(2,1)S(1)}, bf16[32,256]{1,0:T(8,128)(2,1)S(1)}, u32[]{:S(2)}, u32[]{:S(2)}) collective-permute-start(bf16[32,256]{1,0:T(8,128)(2,1)S(1)} %get-tuple-element.338), channel_id=1, source_target_pairs={{0,8},{8,16},{16,24},{24,32},{32,40},{40,48},{48,56},{56,64},{64,7... | collective-permute-start | bytes 49160 | tf_op jit(solution)/shard_map/ppermute | solution.py:21
  112.1 7.2 %collective-permute-start.9 = (bf16[32,256]{1,0:T(8,128)(2,1)S(1)}, bf16[32,256]{1,0:T(8,128)(2,1)S(1)}, u32[]{:S(2)}, u32[]{:S(2)}) collective-permute-start(bf16[32,256]{1,0:T(8,128)(2,1)S(1)} %get-tuple-element.339), channel_id=1, source_target_pairs={{8,0},{16,8},{24,16},{32,24},{40,32},{48,40},{56,48},{64,56},{72,6... | collective-permute-start | bytes 49160 | tf_op jit(solution)/shard_map/ppermute | solution.py:23
  146.8 7.9 %collective-permute-start.10 = (f32[32,256]{1,0:T(8,128)S(1)}, f32[32,256]{1,0:T(8,128)S(1)}, u32[]{:S(2)}, u32[]{:S(2)}) collective-permute-start(f32[32,256]{1,0:T(8,128)S(1)} %get-tuple-element.295), channel_id=1, source_target_pairs={{0,8},{8,16},{16,24},{24,32},{32,40},{40,48},{48,56},{56,64},{64,7... | collective-permute-start | bytes 98312 | tf_op jit(solution)/shard_map/ppermute | solution.py:21
  148.7 7.3 %collective-permute-start.11 = (f32[32,256]{1,0:T(8,128)S(1)}, f32[32,256]{1,0:T(8,128)S(1)}, u32[]{:S(2)}, u32[]{:S(2)}) collective-permute-start(f32[32,256]{1,0:T(8,128)S(1)} %get-tuple-element.294), channel_id=1, source_target_pairs={{8,0},{16,8},{24,16},{32,24},{40,32},{48,40},{56,48},{64,56},{72,6... | collective-permute-start | bytes 98312 | tf_op jit(solution)/shard_map/ppermute | solution.py:23
  157.9 7.7 %collective-permute-start.12 = (bf16[32,256]{1,0:T(8,128)(2,1)S(1)}, bf16[32,256]{1,0:T(8,128)(2,1)S(1)}, u32[]{:S(2)}, u32[]{:S(2)}) collective-permute-start(bf16[32,256]{1,0:T(8,128)(2,1)S(1)} %get-tuple-element.336), channel_id=1, source_target_pairs={{0,8},{8,16},{16,24},{24,32},{32,40},{40,48},{48,56},{56,64},{64,7... | collective-permute-start | bytes 49160 | tf_op jit(solution)/shard_map/ppermute | solution.py:21
  159.8 7.2 %collective-permute-start.13 = (bf16[32,256]{1,0:T(8,128)(2,1)S(1)}, bf16[32,256]{1,0:T(8,128)(2,1)S(1)}, u32[]{:S(2)}, u32[]{:S(2)}) collective-permute-start(bf16[32,256]{1,0:T(8,128)(2,1)S(1)} %get-tuple-element.337), channel_id=1, source_target_pairs={{8,0},{16,8},{24,16},{32,24},{40,32},{48,40},{56,48},{64,56},{72,6... | collective-permute-start | bytes 49160 | tf_op jit(solution)/shard_map/ppermute | solution.py:23
  194.5 7.7 %collective-permute-start.14 = (f32[32,256]{1,0:T(8,128)S(1)}, f32[32,256]{1,0:T(8,128)S(1)}, u32[]{:S(2)}, u32[]{:S(2)}) collective-permute-start(f32[32,256]{1,0:T(8,128)S(1)} %get-tuple-element.293), channel_id=1, source_target_pairs={{0,8},{8,16},{16,24},{24,32},{32,40},{40,48},{48,56},{56,64},{64,7... | collective-permute-start | bytes 98312 | tf_op jit(solution)/shard_map/ppermute | solution.py:21
  196.4 7.3 %collective-permute-start.15 = (f32[32,256]{1,0:T(8,128)S(1)}, f32[32,256]{1,0:T(8,128)S(1)}, u32[]{:S(2)}, u32[]{:S(2)}) collective-permute-start(f32[32,256]{1,0:T(8,128)S(1)} %get-tuple-element.292), channel_id=1, source_target_pairs={{8,0},{16,8},{24,16},{32,24},{40,32},{48,40},{56,48},{64,56},{72,6... | collective-permute-start | bytes 98312 | tf_op jit(solution)/shard_map/ppermute | solution.py:23
  285.4 9.7 %collective-permute-start.16 = (bf16[256,256]{1,0:T(8,128)(2,1)S(1)}, bf16[256,256]{1,0:T(8,128)(2,1)S(1)}, u32[]{:S(2)}, u32[]{:S(2)}) collective-permute-start(bf16[256,256]{1,0:T(8,128)(2,1)S(1)} %fusion.143), channel_id=1, source_target_pairs={{0,8},{8,0},{16,24},{24,16},{32,40},{40,32},{48,56},{56,48},{64,72... | collective-permute-start | bytes 393224 | tf_op jit(solution)/shard_map/ppermute | solution.py:33
  331.8 5.8 %collective-permute-start.17 = (bf16[256,256]{1,0:T(8,128)(2,1)S(1)}, bf16[256,256]{1,0:T(8,128)(2,1)S(1)}, u32[]{:S(2)}, u32[]{:S(2)}) collective-permute-start(bf16[256,256]{1,0:T(8,128)(2,1)S(1)} %fusion.145), channel_id=1, source_target_pairs={{0,16},{8,24},{16,0},{24,8},{32,48},{40,56},{48,32},{56,40},{64,80... | collective-permute-start | bytes 393224 | tf_op jit(solution)/shard_map/ppermute | solution.py:33
  374.4 7.0 %collective-permute-start.18 = (bf16[256,256]{1,0:T(8,128)(2,1)S(1)}, bf16[256,256]{1,0:T(8,128)(2,1)S(1)}, u32[]{:S(2)}, u32[]{:S(2)}) collective-permute-start(bf16[256,256]{1,0:T(8,128)(2,1)S(1)} %fusion.147), channel_id=1, source_target_pairs={{0,32},{8,40},{16,48},{24,56},{32,0},{40,8},{48,16},{56,24},{64,96... | collective-permute-start | bytes 393224 | tf_op jit(solution)/shard_map/ppermute | solution.py:33
  418.2 5.2 collective-permute-start.19
  423.6 103.9 %copy-start = (bf16[256,2048]{1,0:T(8,128)(2,1)S(1)}, bf16[256,2048]{1,0:T(8,128)(2,1)}, u32[]{:S(2)}) copy-start(bf16[256,2048]{1,0:T(8,128)(2,1)} %all-gather.2.cloned.1.call-done) | copy-start | bytes 3145732
  460.2 6.8 %collective-permute-start.20 = (bf16[256,256]{1,0:T(8,128)(2,1)S(1)}, bf16[256,256]{1,0:T(8,128)(2,1)S(1)}, u32[]{:S(2)}, u32[]{:S(2)}) collective-permute-start(bf16[256,256]{1,0:T(8,128)(2,1)S(1)} %fusion.151), channel_id=1, source_target_pairs={{0,128},{8,136},{16,144},{24,152},{32,160},{40,168},{48,176},{56,1... | collective-permute-start | bytes 393224 | tf_op jit(solution)/shard_map/ppermute | solution.py:33
Sparse Core Ops, SparseCore 0:
  205.6 41.7 all-gather.1
where the time goes:
time: 549 us; the launch traced here: 538 us
  other arithmetic  235 us (43%)
  matrix products  121 us (22%)
  starting transfers between devices  78.5 us (14%)
  waiting for transfers between devices  69.1 us (13%)
  between operations  22.1 us (4%)
  local copies, waits for them, and re-layouts  10.9 us (2%)
    another operation x35, other arithmetic, per_device(): factor = jnp.linalg.cholesky(gram_of(factor) + gram_of(partner))  173 us
    dot_general x32, matrix products, add_cell(): cell_terms = jnp.dot(pieces, cell_block, preferred_element_type=jnp.float32)  68.5 us
    ppermute x8, starting transfers between devices, extended_2(): lax.ppermute(head, axis, [((i + 1) % count, i) for i in range(ends)])  46.3 us
    all_gather x1, waiting for transfers between devices, per_device(): lax.all_gather(current.astype(jnp.bfloat16), 'orb', axis=0, tiled=True)  41.9 us
    dot_general x36, matrix products, spread_back(): lax.dot_general(three_parts(values), table, (((1,), (1,)), ((), ())), pre...  38.8 us
    another operation x6, other arithmetic, per_device(): factor = jnp.linalg.cholesky(gram_of(gathered))  33.9 us
    another operation x3, other arithmetic, forward_solve(): lax.linalg.triangular_solve(factor, values, left_side=True, lower=True)  19.7 us
    ppermute x5, starting transfers between devices, partner_2(): return lax.ppermute(value, axis, pairs)  16.8 us
  transfers between devices with their start and end apart: 22, of which 14 were waited for; matrix products, arithmetic and copies ran while one was open for 0% of the time, Pallas kernels for 0%

commit v1 on v0

v1 whole, which is shorter than its diff:
```python
import functools
import math

import jax
import jax.numpy as jnp
from jax import lax
from jax.experimental import pallas as pl
from jax.experimental.pallas import tpu as pltpu
from jax.sharding import PartitionSpec as P

MESH = pl.DeviceIdType.MESH
F32, BF16 = jnp.float32, jnp.bfloat16
HIGHEST = lax.Precision.HIGHEST
NT = (((1,), (1,)), ((), ()))
TN = (((0,), (0,)), ((), ()))

DEGREE = 4
CELLS = 8
LOCAL = 512
ROWS = 32
OWN = 2048
FACE = 256
BLOCKS = 8
SLABS = 32
SIDE = 4
PIECES = 4
PIECE = OWN // PIECES
HALF = ROWS // 2
ALL = ROWS * BLOCKS


def one_hot(first, wanted, rows):
    numbers = lax.broadcasted_iota(jnp.int32, (rows, wanted.shape[1]), 0)
    return jnp.where(numbers == wanted - first, 1.0, 0.0).astype(BF16)


def eliminate(block):
    row_id = lax.broadcasted_iota(jnp.int32, (ROWS, ROWS), 0)
    column_id = lax.broadcasted_iota(jnp.int32, (ROWS, ROWS), 1)
    work = jnp.concatenate([block, (row_id == column_id).astype(F32)], axis=1)
    below = lax.broadcasted_iota(jnp.int32, (ROWS, 1), 0)
    for j in range(ROWS):
        scaled = work[j : j + 1, :] / work[j : j + 1, j : j + 1]
        work = work - jnp.where(below > j, work[:, j : j + 1], 0.0) * scaled
    pivots = jnp.sum(jnp.where(row_id == column_id, work[:, :ROWS], 0.0), axis=1, keepdims=True)
    return work[:, ROWS:] * lax.rsqrt(pivots)


def invert_factor(gram, inverse):
    lane = lax.broadcasted_iota(jnp.int32, (ROWS, ALL), 1)
    row = lax.broadcasted_iota(jnp.int32, (ROWS, ALL), 0)
    for b in range(BLOCKS):
        low, high = b * ROWS, (b + 1) * ROWS
        diagonal = eliminate(gram[low:high, low:high])
        here = (lane >= low) & (lane < high)
        strip = jnp.where(here, (lane - low == row).astype(F32), gram[low:high, :])
        strip = jnp.dot(diagonal, strip, precision=HIGHEST, preferred_element_type=F32)
        inverse[b] = jnp.where(lane < high, strip, 0.0)
        if b < BLOCKS - 1:
            update = lax.dot_general(
                strip[:, high:], strip, TN, precision=HIGHEST, preferred_element_type=F32
            )
            rest = gram[high:, :]
            lanes = lax.broadcasted_iota(jnp.int32, rest.shape, 1)
            gram[high:, :] = jnp.where((lanes >= low) & (lanes < high), 0.0, rest) - update


def kernel(
    orbitals, connectivity, faces, matrices_hbm, out,
    picker, face_table, matrices, field_a, field_b, rounded, pieces, terms,
    halo, halo_out, back, back_out, blocks, halves, half_in, along_x, along_y, rows_all,
    gram, inverse,
    load_sem, halo_ssem, halo_rsem, back_ssem, back_rsem, ring_ssem, ring_rsem,
    core_ssem, core_rsem, x_ssem, x_rsem, y_ssem, y_rsem, z_ssem, z_rsem, pair_ssem, pair_rsem,
):
    s, o = lax.axis_index("slab"), lax.axis_index("orb")
    core, y, x = lax.rem(s, 2), lax.rem(s // 2, SIDE), s // (2 * SIDE)
    other_core = s + 1 - 2 * core

    load = pltpu.make_async_copy(matrices_hbm, matrices, load_sem)
    load.start()

    def slab_of(x_at, y_at, core_at):
        return (x_at * SIDE + y_at) * 2 + core_at

    def copy(source, target, ssem, rsem, **device):
        return pltpu.make_async_remote_copy(
            src_ref=source, dst_ref=target, send_sem=ssem, recv_sem=rsem,
            device_id=device, device_id_type=MESH,
        )

    up, down = lax.rem(s + 1, SLABS), lax.rem(s + SLABS - 1, SLABS)
    has = (s > 0, s < SLABS - 1)
    neighbour = (down, up)

    halo[...] = jnp.zeros_like(halo)
    back[...] = jnp.zeros_like(back)

    barrier = pltpu.get_barrier_semaphore()
    for d in range(1, BLOCKS):
        pl.semaphore_signal(
            barrier, inc=1, device_id={"orb": lax.rem(o + d, BLOCKS)}, device_id_type=MESH
        )
    for d in range(1, SIDE):
        for there in (
            slab_of(lax.rem(x + d, SIDE), y, core),
            slab_of(x, lax.rem(y + d, SIDE), core),
        ):
            pl.semaphore_signal(barrier, inc=1, device_id={"slab": there}, device_id_type=MESH)
    for there in neighbour:
        pl.semaphore_signal(barrier, inc=1, device_id={"slab": there}, device_id_type=MESH)

    face_table[...] = one_hot(0, faces[...], OWN)
    field_a[...] = orbitals[...]
    rounded[...] = orbitals[...].astype(BF16)

    pl.semaphore_wait(barrier, BLOCKS - 1 + 2 * (SIDE - 1) + 2)

    def exchange(k, sent, received, ssem, rsem):
        return [
            copy(
                sent.at[k, side], received.at[k, 1 - side],
                ssem.at[k, side], rsem.at[k, 1 - side], slab=neighbour[side],
            )
            for side in range(2)
        ]

    def start_both(copies):
        for side in range(2):
            pl.when(has[side])(copies[side].start)

    def land_both(copies):
        for side in range(2):
            pl.when(has[side])(copies[1 - side].wait_recv)

    def leave_both(copies):
        for side in range(2):
            pl.when(has[side])(copies[side].wait_send)

    def send_faces(k):
        values = jnp.dot(rounded[...], face_table[...], preferred_element_type=F32).astype(BF16)
        halo_out[k, 0] = values[:, :FACE]
        halo_out[k, 1] = values[:, FACE:]
        copies = exchange(k, halo_out, halo, halo_ssem, halo_rsem)
        start_both(copies)
        return copies

    fields = [field_a, field_b]
    for k in range(DEGREE):
        halo_copies = send_faces(k)
        if k == 0:

            def build(c, _):
                wanted = connectivity[pl.ds(c, 1), :]
                for t in range(OWN // FACE):
                    picker[c, t * FACE : (t + 1) * FACE, :] = one_hot(FACE + t * FACE, wanted, FACE)
                picker[c, OWN : OWN + FACE, :] = one_hot(0, wanted, FACE)
                picker[c, OWN + FACE :, :] = one_hot(OWN + FACE, wanted, FACE)
                return 0

            lax.fori_loop(0, CELLS, build, 0)

        def gather_own(c, _):
            pieces[c] = jnp.dot(
                rounded[...], picker[c, :OWN, :], preferred_element_type=F32
            ).astype(BF16)
            return 0

        lax.fori_loop(0, CELLS, gather_own, 0)
        if k == 0:
            load.wait()
        land_both(halo_copies)
        from_sides = jnp.concatenate([halo[k, 0], halo[k, 1]], axis=1)

        def cell(c, face_sum):
            shared = picker[c, OWN:, :]
            values = pieces[c].astype(F32) + jnp.dot(
                from_sides, shared, preferred_element_type=F32
            )
            term = jnp.dot(
                values.astype(BF16), matrices[c], preferred_element_type=F32
            ).astype(BF16)
            terms[c] = term
            return face_sum + lax.dot_general(term, shared, NT, preferred_element_type=F32)

        face_sum = lax.fori_loop(0, CELLS, cell, jnp.zeros((ROWS, 2 * FACE), F32))
        back_out[k, 0] = face_sum[:, :FACE].astype(BF16)
        back_out[k, 1] = face_sum[:, FACE:].astype(BF16)
        back_copies = exchange(k, back_out, back, back_ssem, back_rsem)
        start_both(back_copies)

        target = fields[(k + 1) % 2]

        def scatter_own(t, _):
            columns = pl.ds(pl.multiple_of(t * FACE, FACE), FACE)
            total = jnp.zeros((ROWS, FACE), F32)
            for c in range(CELLS):
                total += lax.dot_general(
                    terms[c], picker[c, columns, :], NT, preferred_element_type=F32
                )
            if k == 0:
                target[:, columns] = total
            else:
                target[:, columns] = 2.0 * total - target[:, columns]
            return 0

        lax.fori_loop(0, OWN // FACE, scatter_own, 0)
        land_both(back_copies)
        incoming = jnp.concatenate([back[k, 0], back[k, 1]], axis=1)
        added = lax.dot_general(incoming, face_table[...], NT, preferred_element_type=F32)
        current = target[...] + (added if k == 0 else 2.0 * added)
        if k < DEGREE - 1:
            target[...] = current
            rounded[...] = current.astype(BF16)
        else:
            for p in range(PIECES):
                blocks[o, p] = current[:, p * PIECE : (p + 1) * PIECE].astype(BF16)
        leave_both(halo_copies)
        leave_both(back_copies)

    def turn(at):
        return lax.rem(at + BLOCKS, BLOCKS)

    ways = (1, -1)
    far = BLOCKS // 2

    def moves(way, d, p):
        return d < far or (d == far and (p < PIECES // 2) == (way == 0))

    def ring(way, d, p):
        step = ways[way]
        held = blocks.at[turn(o - step * (d - 1)), p]
        return copy(
            held, held, ring_ssem.at[way, d - 1, p], ring_rsem.at[way, d - 1, p],
            orb=turn(o + step),
        )

    sent = []
    for d in range(1, far + 2):
        for p in range(PIECES):
            for way in range(2):
                if d > 1 and moves(way, d - 1, p):
                    ring(way, d - 1, p).wait_recv()
                if d <= far and moves(way, d, p):
                    one = ring(way, d, p)
                    one.start()
                    sent.append(one)

    strip = jnp.zeros((ROWS, ALL), F32)
    for p in range(PIECES):
        strip += lax.dot_general(
            blocks[o, p], blocks[:, p].reshape(ALL, PIECE), NT, preferred_element_type=F32
        )
    halves[0] = strip[:HALF]
    halves[1] = strip[HALF:]

    one = copy(halves.at[1 - core], half_in, core_ssem, core_rsem, slab=other_core)
    one.start()
    one.wait()
    along_x[0] = halves[core] + half_in[...]
    copies = [
        copy(
            along_x.at[0], along_x.at[d], x_ssem.at[d], x_rsem.at[d],
            slab=slab_of(lax.rem(x + d, SIDE), y, core),
        )
        for d in range(1, SIDE)
    ]
    for one in copies:
        one.start()
    for one in copies:
        one.wait()
    along_y[0] = (along_x[0] + along_x[1]) + (along_x[2] + along_x[3])
    copies = [
        copy(
            along_y.at[0], along_y.at[d], y_ssem.at[d], y_rsem.at[d],
            slab=slab_of(x, lax.rem(y + d, SIDE), core),
        )
        for d in range(1, SIDE)
    ]
    for one in copies:
        one.start()
    for one in copies:
        one.wait()
    rows_all[core, o] = (along_y[0] + along_y[1]) + (along_y[2] + along_y[3])

    def pair(k):
        held = rows_all.at[core, k]
        return copy(held, held, pair_ssem.at[k], pair_rsem.at[k], slab=other_core)

    copies = [
        copy(
            rows_all.at[core, o], rows_all.at[core, o], z_ssem.at[d], z_rsem.at[d],
            orb=turn(o + d),
        )
        for d in range(1, BLOCKS)
    ]
    for d in (4, 3, 5, 2, 6, 1, 7):
        copies[d - 1].start()
    pair(o).start()
    for d in (1, 7, 2, 6, 3, 5, 4):
        copies[d - 1].wait_recv()
        pair(turn(o - d)).start()
    for k in range(BLOCKS):
        pair(k).wait()
    for one in copies + sent:
        one.wait_send()

    for k in range(BLOCKS):
        for h in range(2):
            first = k * ROWS + h * HALF
            gram[first : first + HALF, :] = rows_all[h, k]
    invert_factor(gram, inverse)

    weights = inverse[o] * math.sqrt(OWN * SLABS)
    upper = weights.astype(BF16)
    lower = (weights - upper.astype(F32)).astype(BF16)
    weights = jnp.concatenate([upper, lower], axis=0)
    for p in range(PIECES):
        both = jnp.dot(weights, blocks[:, p].reshape(ALL, PIECE), preferred_element_type=F32)
        out[:, p * PIECE : (p + 1) * PIECE] = both[:ROWS] + both[ROWS:]


def per_device(orbitals, cell_matrices, connectivity, face_lower, face_upper):
    faces = jnp.concatenate([face_lower, face_upper], axis=0)[None, :]
    vmem = pl.BlockSpec(memory_space=pltpu.VMEM)
    dma = pltpu.SemaphoreType.DMA
    return pl.pallas_call(
        kernel,
        out_shape=jax.ShapeDtypeStruct((ROWS, OWN), F32),
        in_specs=[vmem, vmem, vmem, pl.BlockSpec(memory_space=pl.ANY)],
        out_specs=vmem,
        scratch_shapes=[
            pltpu.VMEM((CELLS, OWN + 2 * FACE, LOCAL), BF16),
            pltpu.VMEM((OWN, 2 * FACE), BF16),
            pltpu.VMEM((CELLS, LOCAL, LOCAL), BF16),
            pltpu.VMEM((ROWS, OWN), F32),
            pltpu.VMEM((ROWS, OWN), F32),
            pltpu.VMEM((ROWS, OWN), BF16),
            pltpu.VMEM((CELLS, ROWS, LOCAL), BF16),
            pltpu.VMEM((CELLS, ROWS, LOCAL), BF16),
            pltpu.VMEM((DEGREE, 2, ROWS, FACE), BF16),
            pltpu.VMEM((DEGREE, 2, ROWS, FACE), BF16),
            pltpu.VMEM((DEGREE, 2, ROWS, FACE), BF16),
            pltpu.VMEM((DEGREE, 2, ROWS, FACE), BF16),
            pltpu.VMEM((BLOCKS, PIECES, ROWS, PIECE), BF16),
            pltpu.VMEM((2, HALF, ALL), F32),
            pltpu.VMEM((HALF, ALL), F32),
            pltpu.VMEM((SIDE, HALF, ALL), F32),
            pltpu.VMEM((SIDE, HALF, ALL), F32),
            pltpu.VMEM((2, BLOCKS, HALF, ALL), F32),
            pltpu.VMEM((ALL, ALL), F32),
            pltpu.VMEM((BLOCKS, ROWS, ALL), F32),
            dma,
            dma((DEGREE, 2)), dma((DEGREE, 2)), dma((DEGREE, 2)), dma((DEGREE, 2)),
            dma((2, BLOCKS // 2, PIECES)), dma((2, BLOCKS // 2, PIECES)),
            dma, dma,
            dma((SIDE,)), dma((SIDE,)), dma((SIDE,)), dma((SIDE,)),
            dma((BLOCKS,)), dma((BLOCKS,)), dma((BLOCKS,)), dma((BLOCKS,)),
        ],
        compiler_params=pltpu.CompilerParams(collective_id=0, has_side_effects=True),
        name="filter_and_orthonormalize",
    )(orbitals, connectivity, faces, cell_matrices)


def solution(mesh):
    in_specs = (P("orb", "slab"), P("slab", None, None), P("slab", None), P("slab"), P("slab"))
    return jax.shard_map(
        per_device, mesh=mesh, in_specs=in_specs, out_specs=P("orb", "slab"), check_vma=False
    )
```

time: 549 us -> 138 us (0.25)
  the two profiles are of different devices: /device:TPU:2 before, /device:TPU:1 now
where the time goes in v1:
time: 138 us
  Pallas kernels  135 us (98%)
  local copies, waits for them, and re-layouts  1.67 us (1%)
    pallas_call x1, Pallas kernels, per_device(): pl.pallas_call(kernel, out_shape=jax.ShapeDtypeStruct((ROWS, OWN), F32),...  135 us

profile of v1, /device:TPU:1, one launch (start us, length us, event | category | flops | bytes accessed | tf_op | source)
XLA Modules:
  0.0 138.1 jit_solution(16489931718173521953)
XLA Ops:
  0.0 1.3 pad_add_fusion
  1.3 135.1 %filter_and_orthonormalize.1 = f32[32,2048]{1,0:T(8,128)} custom-call(f32[32,2048]{1,0:T(8,128)} %orbitals.1, s32[8,512]{1,0:T(8,128)} %connectivity.1, s32[1,512]{1,0:T(1,128)} %bitcast.1, bf16[8,512,512]{2,1,0:T(8,128)(2,1)} %matrices_hbm.1), custom_call_target="tpu_custom_call" | custom-call | tf_op jit(solution)/shard_map/filter_and_orthonormalize/pallas_call | solution.py:327
  136.4 1.7 %copy.7 = f32[32,2048]{1,0:T(8,128)} copy(f32[32,2048]{1,0:T(8,128)} %filter_and_orthonormalize.1) | data formatting | bytes 524288

commit v2 on v1

--- a/solution.py
+++ b/solution.py
@@ -10,7 +10,6 @@
 
 MESH = pl.DeviceIdType.MESH
 F32, BF16 = jnp.float32, jnp.bfloat16
-HIGHEST = lax.Precision.HIGHEST
 NT = (((1,), (1,)), ((), ()))
 TN = (((0,), (0,)), ((), ()))
 
@@ -18,8 +17,12 @@
 CELLS = 8
 LOCAL = 512
 ROWS = 32
+PACK = 16
+SUB = 8
+LANES = 128
 OWN = 2048
 FACE = 256
+EXT_TILES = 20
 BLOCKS = 8
 SLABS = 32
 SIDE = 4
@@ -29,45 +32,129 @@
 ALL = ROWS * BLOCKS
 
 
-def one_hot(first, wanted, rows):
-    numbers = lax.broadcasted_iota(jnp.int32, (rows, wanted.shape[1]), 0)
-    return jnp.where(numbers == wanted - first, 1.0, 0.0).astype(BF16)
-
-
-def eliminate(block):
-    row_id = lax.broadcasted_iota(jnp.int32, (ROWS, ROWS), 0)
-    column_id = lax.broadcasted_iota(jnp.int32, (ROWS, ROWS), 1)
-    work = jnp.concatenate([block, (row_id == column_id).astype(F32)], axis=1)
-    below = lax.broadcasted_iota(jnp.int32, (ROWS, 1), 0)
-    for j in range(ROWS):
-        scaled = work[j : j + 1, :] / work[j : j + 1, j : j + 1]
-        work = work - jnp.where(below > j, work[:, j : j + 1], 0.0) * scaled
-    pivots = jnp.sum(jnp.where(row_id == column_id, work[:, :ROWS], 0.0), axis=1, keepdims=True)
-    return work[:, ROWS:] * lax.rsqrt(pivots)
+def pick(tile, index):
+    numbers = lax.GatherDimensionNumbers(
+        offset_dims=(), collapsed_slice_dims=(1,), start_index_map=(1,),
+        operand_batching_dims=(0,), start_indices_batching_dims=(0,),
+    )
+    return lax.gather(
+        tile, index[..., None], numbers, (1, 1), mode=lax.GatherScatterMode.PROMISE_IN_BOUNDS
+    )
+
+
+def pick_among(tiles, lane_at, tile_at, start):
+    for number, tile in tiles:
+        start = jnp.where(tile_at == number, pick(tile, lane_at), start)
+    return start
+
+
+def spread(row):
+    return jnp.broadcast_to(row, (PACK, LANES)).astype(jnp.int16)
+
+
+def split_tables(wanted, table):
+    for j in range(LOCAL // LANES):
+        part = wanted[:, j * LANES : (j + 1) * LANES]
+        table[j, 0] = spread(lax.rem(part, LANES))
+        table[j, 1] = spread(part // LANES)
+
+
+def inverse_tables(wanted, tiles, table):
+    number = lax.broadcasted_iota(jnp.int32, (1, LOCAL), 1)
+    at_tile = lax.broadcasted_iota(jnp.int32, (ROWS, LOCAL), 0) == wanted // LANES
+    lanes = jnp.where(at_tile, lax.rem(number, LANES).astype(F32), 0.0)
+    numbers = jnp.where(at_tile, (number // LANES + 1).astype(F32), 0.0)
+    at_lane = lax.broadcasted_iota(jnp.int32, (LANES, LOCAL), 0) == lax.rem(wanted, LANES)
+    found = lax.dot_general(
+        jnp.concatenate([lanes, numbers], axis=0).astype(BF16),
+        jnp.where(at_lane, 1.0, 0.0).astype(BF16),
+        NT, preferred_element_type=F32,
+    ).astype(jnp.int32)
+    for t in range(tiles):
+        table[t, 0] = spread(found[t : t + 1])
+        table[t, 1] = spread(found[ROWS + t : ROWS + t + 1] - 1)
+
+
+def split3(x):
+    high = x.astype(BF16)
+    rest = x - high.astype(F32)
+    middle = rest.astype(BF16)
+    low = (rest - middle.astype(F32)).astype(BF16)
+    return high, middle, low
 
 
 def invert_factor(gram, inverse):
-    lane = lax.broadcasted_iota(jnp.int32, (ROWS, ALL), 1)
-    row = lax.broadcasted_iota(jnp.int32, (ROWS, ALL), 0)
+    groups = ROWS // SUB
+    sub = lax.broadcasted_iota(jnp.int32, (SUB, LANES), 0)
+    lane = lax.broadcasted_iota(jnp.int32, (SUB, LANES), 1)
+    wide = lax.broadcasted_iota(jnp.int32, (ROWS, ALL), 1)
+    zero = jnp.zeros((SUB, LANES), F32)
+
+    def row_of(tile, j):
+        return jnp.broadcast_to(tile[j : j + 1, :], (SUB, LANES))
+
+    def column_of(tile, j):
+        return jnp.broadcast_to(tile[:, j : j + 1], (SUB, LANES))
+
+    strip = gram[:ROWS, :]
     for b in range(BLOCKS):
         low, high = b * ROWS, (b + 1) * ROWS
-        diagonal = eliminate(gram[low:high, low:high])
-        here = (lane >= low) & (lane < high)
-        strip = jnp.where(here, (lane - low == row).astype(F32), gram[low:high, :])
-        strip = jnp.dot(diagonal, strip, precision=HIGHEST, preferred_element_type=F32)
-        inverse[b] = jnp.where(lane < high, strip, 0.0)
+        home, shift = low // LANES, low % LANES
+        tiles = [
+            [strip[g * SUB : (g + 1) * SUB, h * LANES : (h + 1) * LANES] for h in range(2)]
+            + [jnp.where(lane - shift == sub + g * SUB, 1.0, 0.0)]
+            for g in range(groups)
+        ]
+        scales = []
+        for q in range(groups):
+            columns = [
+                [column_of(tiles[g][home], shift + q * SUB + k) for g in range(q, groups)]
+                for k in range(SUB)
+            ]
+            pivots = zero
+            for j in range(SUB):
+                pivot = row_of(columns[j][0], j)
+                pivots = jnp.where(sub == j, pivot, pivots)
+                inv = 1.0 / pivot
+                factors = [jnp.where(sub > j, columns[j][0], 0.0)] + columns[j][1:]
+                for k in range(j + 1, SUB):
+                    scaled = row_of(columns[k][0], j) * inv
+                    columns[k] = [c - m * scaled for c, m in zip(columns[k], factors)]
+                rows = [row_of(t, j) * inv for t in tiles[q]]
+                for g in range(q, groups):
+                    tiles[g] = [t - factors[g - q] * r for t, r in zip(tiles[g], rows)]
+            scales.append(lax.rsqrt(pivots))
+        tiles = [[t * scales[g] for t in tiles[g]] for g in range(groups)]
+        parts = []
+        for h in range(2):
+            part = jnp.concatenate([tiles[g][h] for g in range(groups)], axis=0)
+            if h == home:
+                unit = jnp.concatenate([tiles[g][2] for g in range(groups)], axis=0)
+                at = lax.broadcasted_iota(jnp.int32, (ROWS, LANES), 1)
+                part = jnp.where((at >= shift) & (at < shift + ROWS), unit, part)
+            parts.append(part)
+        strip = jnp.concatenate(parts, axis=1)
+        inverse[b] = jnp.where(wide < high, strip, 0.0)
         if b < BLOCKS - 1:
-            update = lax.dot_general(
-                strip[:, high:], strip, TN, precision=HIGHEST, preferred_element_type=F32
-            )
-            rest = gram[high:, :]
-            lanes = lax.broadcasted_iota(jnp.int32, rest.shape, 1)
-            gram[high:, :] = jnp.where((lanes >= low) & (lanes < high), 0.0, rest) - update
+            h0, m0, l0 = split3(strip)
+            right = jnp.concatenate([h0, m0, h0, m0, l0, h0], axis=0)
+            left = jnp.concatenate([h0, h0, m0, m0, h0, l0], axis=0)[:, high:]
+
+            def updated(rest, first, last):
+                update = lax.dot_general(
+                    left[:, first - high : last - high], right, TN, preferred_element_type=F32
+                )
+                at = lax.broadcasted_iota(jnp.int32, rest.shape, 1)
+                return jnp.where((at >= low) & (at < high), 0.0, rest) - update
+
+            strip = updated(gram[high : high + ROWS, :], high, high + ROWS)
+            if b < BLOCKS - 2:
+                gram[high + ROWS :, :] = updated(gram[high + ROWS :, :], high + ROWS, ALL)
 
 
 def kernel(
     orbitals, connectivity, faces, matrices_hbm, out,
-    picker, face_table, matrices, field_a, field_b, rounded, pieces, terms,
+    gather_at, scatter_at, face_from, face_to, matrices, field_a, field_b, rounded, pieces, terms,
     halo, halo_out, back, back_out, blocks, halves, half_in, along_x, along_y, rows_all,
     gram, inverse,
     load_sem, halo_ssem, halo_rsem, back_ssem, back_rsem, ring_ssem, ring_rsem,
@@ -110,9 +197,10 @@
     for there in neighbour:
         pl.semaphore_signal(barrier, inc=1, device_id={"slab": there}, device_id_type=MESH)
 
-    face_table[...] = one_hot(0, faces[...], OWN)
     field_a[...] = orbitals[...]
     rounded[...] = orbitals[...].astype(BF16)
+    split_tables(faces[...], face_from)
+    inverse_tables(faces[...], OWN // LANES, face_to)
 
     pl.semaphore_wait(barrier, BLOCKS - 1 + 2 * (SIDE - 1) + 2)
 
@@ -137,84 +225,116 @@
         for side in range(2):
             pl.when(has[side])(copies[side].wait_send)
 
+    groups = [slice(g * PACK, (g + 1) * PACK) for g in range(ROWS // PACK)]
+    local_tiles, side_tiles, own_tiles = LOCAL // LANES, FACE // LANES, OWN // LANES
+    nothing = jnp.zeros((PACK, LANES), BF16)
+
+    def span(t, width=LANES):
+        return slice(t * width, (t + 1) * width)
+
+    def side_of(buffer, k, t, g):
+        return buffer[k, t // side_tiles, groups[g], span(t % side_tiles)]
+
     def send_faces(k):
-        values = jnp.dot(rounded[...], face_table[...], preferred_element_type=F32).astype(BF16)
-        halo_out[k, 0] = values[:, :FACE]
-        halo_out[k, 1] = values[:, FACE:]
+        for j in range(2 * side_tiles):
+            for rows in groups:
+                halo_out[k, j // side_tiles, rows, span(j % side_tiles)] = pick_among(
+                    [(t, rounded[rows, span(t)]) for t in range(own_tiles)],
+                    face_from[j, 0], face_from[j, 1], nothing,
+                )
         copies = exchange(k, halo_out, halo, halo_ssem, halo_rsem)
         start_both(copies)
         return copies
+
+    def gathered(t, g):
+        total = jnp.zeros((PACK, LANES), F32)
+        for c in range(CELLS):
+            total += pick_among(
+                [(h, terms[c, groups[g], span(h)]) for h in range(local_tiles)],
+                scatter_at[c, t, 0], scatter_at[c, t, 1], nothing,
+            ).astype(F32)
+        return total
 
     fields = [field_a, field_b]
     for k in range(DEGREE):
         halo_copies = send_faces(k)
         if k == 0:
 
-            def build(c, _):
+            def tables(c, _):
                 wanted = connectivity[pl.ds(c, 1), :]
-                for t in range(OWN // FACE):
-                    picker[c, t * FACE : (t + 1) * FACE, :] = one_hot(FACE + t * FACE, wanted, FACE)
-                picker[c, OWN : OWN + FACE, :] = one_hot(0, wanted, FACE)
-                picker[c, OWN + FACE :, :] = one_hot(OWN + FACE, wanted, FACE)
+                split_tables(wanted, gather_at.at[c])
+                inverse_tables(wanted, EXT_TILES, scatter_at.at[c])
                 return 0
 
-            lax.fori_loop(0, CELLS, build, 0)
-
-        def gather_own(c, _):
-            pieces[c] = jnp.dot(
-                rounded[...], picker[c, :OWN, :], preferred_element_type=F32
-            ).astype(BF16)
+            lax.fori_loop(0, CELLS, tables, 0)
+
+        def gather_own(i, _):
+            for c in (2 * i, 2 * i + 1):
+                for j in range(local_tiles):
+                    for rows in groups:
+                        pieces[c, rows, span(j)] = pick_among(
+                            [(t + side_tiles, rounded[rows, span(t)]) for t in range(own_tiles)],
+                            gather_at[c, j, 0], gather_at[c, j, 1], nothing,
+                        )
             return 0
 
-        lax.fori_loop(0, CELLS, gather_own, 0)
+        lax.fori_loop(0, CELLS // 2, gather_own, 0)
         if k == 0:
             load.wait()
         land_both(halo_copies)
-        from_sides = jnp.concatenate([halo[k, 0], halo[k, 1]], axis=1)
-
-        def cell(c, face_sum):
-            shared = picker[c, OWN:, :]
-            values = pieces[c].astype(F32) + jnp.dot(
-                from_sides, shared, preferred_element_type=F32
-            )
-            term = jnp.dot(
-                values.astype(BF16), matrices[c], preferred_element_type=F32
-            ).astype(BF16)
-            terms[c] = term
-            return face_sum + lax.dot_general(term, shared, NT, preferred_element_type=F32)
-
-        face_sum = lax.fori_loop(0, CELLS, cell, jnp.zeros((ROWS, 2 * FACE), F32))
-        back_out[k, 0] = face_sum[:, :FACE].astype(BF16)
-        back_out[k, 1] = face_sum[:, FACE:].astype(BF16)
+
+        def cell(i, _):
+            for c in (2 * i, 2 * i + 1):
+                for j in range(local_tiles):
+                    for g, rows in enumerate(groups):
+                        pieces[c, rows, span(j)] = pick_among(
+                            [
+                                (t if t < side_tiles else t + own_tiles, side_of(halo, k, t, g))
+                                for t in range(2 * side_tiles)
+                            ],
+                            gather_at[c, j, 0], gather_at[c, j, 1], pieces[c, rows, span(j)],
+                        )
+                terms[c] = jnp.dot(
+                    pieces[c], matrices[c], preferred_element_type=F32
+                ).astype(BF16)
+            return 0
+
+        lax.fori_loop(0, CELLS // 2, cell, 0)
+        for t in range(2 * side_tiles):
+            for g, rows in enumerate(groups):
+                back_out[k, t // side_tiles, rows, span(t % side_tiles)] = gathered(
+                    t if t < side_tiles else t + own_tiles, g
+                ).astype(BF16)
         back_copies = exchange(k, back_out, back, back_ssem, back_rsem)
         start_both(back_copies)
 
         target = fields[(k + 1) % 2]
 
-        def scatter_own(t, _):
-            columns = pl.ds(pl.multiple_of(t * FACE, FACE), FACE)
-            total = jnp.zeros((ROWS, FACE), F32)
-            for c in range(CELLS):
-                total += lax.dot_general(
-                    terms[c], picker[c, columns, :], NT, preferred_element_type=F32
-                )
-            if k == 0:
-                target[:, columns] = total
-            else:
-                target[:, columns] = 2.0 * total - target[:, columns]
+        def scatter_own(i, _):
+            for t in (2 * i, 2 * i + 1):
+                columns = pl.ds(pl.multiple_of(t * LANES, LANES), LANES)
+                for g, rows in enumerate(groups):
+                    total = gathered(t + side_tiles, g)
+                    if k > 0:
+                        total = 2.0 * total - target[rows, columns]
+                    target[rows, columns] = total
             return 0
 
-        lax.fori_loop(0, OWN // FACE, scatter_own, 0)
+        lax.fori_loop(0, own_tiles // 2, scatter_own, 0)
         land_both(back_copies)
-        incoming = jnp.concatenate([back[k, 0], back[k, 1]], axis=1)
-        added = lax.dot_general(incoming, face_table[...], NT, preferred_element_type=F32)
-        current = target[...] + (added if k == 0 else 2.0 * added)
-        if k < DEGREE - 1:
-            target[...] = current
-            rounded[...] = current.astype(BF16)
-        else:
-            for p in range(PIECES):
-                blocks[o, p] = current[:, p * PIECE : (p + 1) * PIECE].astype(BF16)
+        for t in range(own_tiles):
+            for g, rows in enumerate(groups):
+                added = pick_among(
+                    [(h, side_of(back, k, h, g)) for h in range(2 * side_tiles)],
+                    face_to[t, 0], face_to[t, 1], nothing,
+                ).astype(F32)
+                current = target[rows, span(t)] + (added if k == 0 else 2.0 * added)
+                if k < DEGREE - 1:
+                    target[rows, span(t)] = current
+                    rounded[rows, span(t)] = current.astype(BF16)
+                else:
+                    p, q = divmod(t, PIECE // LANES)
+                    blocks[o, p, rows, span(q)] = current.astype(BF16)
         leave_both(halo_copies)
         leave_both(back_copies)
 
@@ -330,8 +450,10 @@
         in_specs=[vmem, vmem, vmem, pl.BlockSpec(memory_space=pl.ANY)],
         out_specs=vmem,
         scratch_shapes=[
-            pltpu.VMEM((CELLS, OWN + 2 * FACE, LOCAL), BF16),
-            pltpu.VMEM((OWN, 2 * FACE), BF16),
+            pltpu.VMEM((CELLS, LOCAL // LANES, 2, PACK, LANES), jnp.int16),
+            pltpu.VMEM((CELLS, EXT_TILES, 2, PACK, LANES), jnp.int16),
+            pltpu.VMEM((LOCAL // LANES, 2, PACK, LANES), jnp.int16),
+            pltpu.VMEM((OWN // LANES, 2, PACK, LANES), jnp.int16),
             pltpu.VMEM((CELLS, LOCAL, LOCAL), BF16),
             pltpu.VMEM((ROWS, OWN), F32),
             pltpu.VMEM((ROWS, OWN), F32),

time: 138 us -> 89.5 us (0.65)
  Pallas kernels: 135 us -> 86.4 us
    pallas_call x1, Pallas kernels: 135 us -> 86.4 us  [per_device(): pl.pallas_call(kernel, out_shape=jax.ShapeDtypeStruct((ROWS, OWN), F32),...]
where the time goes in v2:
time: 89.5 us; the launch traced here: 89.4 us
  Pallas kernels  86.4 us (97%)
  local copies, waits for them, and re-layouts  1.67 us (2%)
  other arithmetic  1.28 us (1%)
    pallas_call x1, Pallas kernels, per_device(): pl.pallas_call(kernel, out_shape=jax.ShapeDtypeStruct((ROWS, OWN), F32),...  86.4 us

profile of v2, /device:TPU:1, one launch (start us, length us, event | category | flops | bytes accessed | tf_op | source)
XLA Modules:
  0.0 89.4 jit_solution(3793976508645650088)
XLA Ops:
  0.0 1.3 %pad_add_fusion = s32[512]{0:T(512)} fusion(s32[256]{0:T(256)} %param.9, s32[256]{0:T(256)} %param.8), kind=kLoop, calls=%fused_computation | loop fusion | flops 512 | bytes 4096 | tf_op jit(solution)/shard_map/concatenate | solution.py:444
  1.3 86.4 %filter_and_orthonormalize.1 = f32[32,2048]{1,0:T(8,128)} custom-call(f32[32,2048]{1,0:T(8,128)} %orbitals.1, s32[8,512]{1,0:T(8,128)} %connectivity.1, s32[1,512]{1,0:T(1,128)} %bitcast.1, bf16[8,512,512]{2,1,0:T(8,128)(2,1)} %matrices_hbm.1), custom_call_target="tpu_custom_call" | custom-call | tf_op jit(solution)/shard_map/filter_and_orthonormalize/pallas_call | solution.py:447
  87.7 1.7 %copy.7 = f32[32,2048]{1,0:T(8,128)} copy(f32[32,2048]{1,0:T(8,128)} %filter_and_orthonormalize.1) | data formatting | bytes 524288

commit v3 on v2

--- a/solution.py
+++ b/solution.py
@@ -22,10 +22,14 @@
 LANES = 128
 OWN = 2048
 FACE = 256
-EXT_TILES = 20
+OWN_TILES = OWN // LANES
+BORDER_TILES = 8
+BORDER = BORDER_TILES * LANES
+TILES = OWN_TILES + BORDER_TILES
 BLOCKS = 8
 SLABS = 32
 SIDE = 4
+STEP_TILES = 4
 PIECES = 4
 PIECE = OWN // PIECES
 HALF = ROWS // 2
@@ -52,24 +56,35 @@
     return jnp.broadcast_to(row, (PACK, LANES)).astype(jnp.int16)
 
 
+def lane_of(position):
+    return jnp.bitwise_and(position, LANES - 1)
+
+
+def tile_of(position):
+    return lax.shift_right_arithmetic(position, 7)
+
+
 def split_tables(wanted, table):
     for j in range(LOCAL // LANES):
         part = wanted[:, j * LANES : (j + 1) * LANES]
-        table[j, 0] = spread(lax.rem(part, LANES))
-        table[j, 1] = spread(part // LANES)
-
-
-def inverse_tables(wanted, tiles, table):
+        table[j, 0] = spread(lane_of(part))
+        table[j, 1] = spread(tile_of(part))
+
+
+def find(wanted):
     number = lax.broadcasted_iota(jnp.int32, (1, LOCAL), 1)
-    at_tile = lax.broadcasted_iota(jnp.int32, (ROWS, LOCAL), 0) == wanted // LANES
-    lanes = jnp.where(at_tile, lax.rem(number, LANES).astype(F32), 0.0)
-    numbers = jnp.where(at_tile, (number // LANES + 1).astype(F32), 0.0)
-    at_lane = lax.broadcasted_iota(jnp.int32, (LANES, LOCAL), 0) == lax.rem(wanted, LANES)
-    found = lax.dot_general(
+    at_tile = lax.broadcasted_iota(jnp.int32, (ROWS, LOCAL), 0) == tile_of(wanted)
+    lanes = jnp.where(at_tile, lane_of(number).astype(F32), 0.0)
+    numbers = jnp.where(at_tile, (tile_of(number) + 1).astype(F32), 0.0)
+    at_lane = lax.broadcasted_iota(jnp.int32, (LANES, LOCAL), 0) == lane_of(wanted)
+    return lax.dot_general(
         jnp.concatenate([lanes, numbers], axis=0).astype(BF16),
         jnp.where(at_lane, 1.0, 0.0).astype(BF16),
         NT, preferred_element_type=F32,
     ).astype(jnp.int32)
+
+
+def inverse_tables(found, tiles, table):
     for t in range(tiles):
         table[t, 0] = spread(found[t : t + 1])
         table[t, 1] = spread(found[ROWS + t : ROWS + t + 1] - 1)
@@ -153,20 +168,18 @@
 
 
 def kernel(
-    orbitals, connectivity, faces, matrices_hbm, out,
-    gather_at, scatter_at, face_from, face_to, matrices, field_a, field_b, rounded, pieces, terms,
-    halo, halo_out, back, back_out, blocks, halves, half_in, along_x, along_y, rows_all,
-    gram, inverse,
-    load_sem, halo_ssem, halo_rsem, back_ssem, back_rsem, ring_ssem, ring_rsem,
+    orbitals, connectivity, lower, upper, matrices_hbm, out,
+    places, gather_at, scatter_at, face_to, matrices, field_a, field_b, border_a, border_b,
+    part, rounded, rounded_border, pieces, terms,
+    first_out, first_in, shared_out, shared_in,
+    blocks, halves, half_in, along_x, along_y, rows_all, gram, inverse,
+    load_sem, first_ssem, first_rsem, shared_ssem, shared_rsem, ring_ssem, ring_rsem,
     core_ssem, core_rsem, x_ssem, x_rsem, y_ssem, y_rsem, z_ssem, z_rsem, pair_ssem, pair_rsem,
 ):
     s, o = lax.axis_index("slab"), lax.axis_index("orb")
     core, y, x = lax.rem(s, 2), lax.rem(s // 2, SIDE), s // (2 * SIDE)
     other_core = s + 1 - 2 * core
 
-    load = pltpu.make_async_copy(matrices_hbm, matrices, load_sem)
-    load.start()
-
     def slab_of(x_at, y_at, core_at):
         return (x_at * SIDE + y_at) * 2 + core_at
 
@@ -180,8 +193,8 @@
     has = (s > 0, s < SLABS - 1)
     neighbour = (down, up)
 
-    halo[...] = jnp.zeros_like(halo)
-    back[...] = jnp.zeros_like(back)
+    first_in[...] = jnp.zeros_like(first_in)
+    shared_in[...] = jnp.zeros_like(shared_in)
 
     barrier = pltpu.get_barrier_semaphore()
     for d in range(1, BLOCKS):
@@ -197,18 +210,60 @@
     for there in neighbour:
         pl.semaphore_signal(barrier, inc=1, device_id={"slab": there}, device_id_type=MESH)
 
+    load = pltpu.make_async_copy(matrices_hbm, matrices, load_sem)
+    load.start()
+
+    groups = [slice(g * PACK, (g + 1) * PACK) for g in range(ROWS // PACK)]
+    local_tiles, side_tiles = LOCAL // LANES, FACE // LANES
+
+    def span(t, width=LANES):
+        return slice(t * width, (t + 1) * width)
+
+    faces = jnp.concatenate([lower[...], upper[...]], axis=1)
+    for j in range(2 * side_tiles):
+        lane_at = jnp.broadcast_to(lane_of(faces[:, span(j)]), (SUB, LANES))
+        tile_at = jnp.broadcast_to(tile_of(faces[:, span(j)]), (SUB, LANES))
+        for g in range(ROWS // SUB):
+            rows = span(g, SUB)
+            values = pick_among(
+                [(t, orbitals[rows, span(t)]) for t in range(OWN_TILES)],
+                lane_at, tile_at, jnp.zeros((SUB, LANES), F32),
+            )
+            border_a[rows, span(j)] = values
+            first_out[j // side_tiles, rows, span(j % side_tiles)] = values
     field_a[...] = orbitals[...]
     rounded[...] = orbitals[...].astype(BF16)
-    split_tables(faces[...], face_from)
-    inverse_tables(faces[...], OWN // LANES, face_to)
+
+    found = find(faces)
+    inverse_tables(found, OWN_TILES, face_to)
+    for j in range(local_tiles):
+        wanted = connectivity[:, span(j)]
+        own = wanted - FACE
+        face = jnp.full((CELLS, LANES), -1, jnp.int32)
+        for t in range(OWN_TILES):
+            row = found[t : t + 1] + LANES * (found[ROWS + t : ROWS + t + 1] - 1)
+            face = pick_among(
+                [(t, jnp.broadcast_to(row, (CELLS, LANES)))], lane_of(own), tile_of(own), face
+            )
+        place = jnp.where(face >= 0, face + OWN, own)
+        place = jnp.where(wanted < FACE, wanted + (OWN + 2 * FACE), place)
+        places[:, span(j)] = jnp.where(wanted >= OWN + FACE, wanted + 2 * FACE, place)
+
+    def tables(c, _):
+        wanted = places[pl.ds(c, 1), :]
+        split_tables(wanted, gather_at.at[c])
+        inverse_tables(find(wanted), TILES, scatter_at.at[c])
+        return 0
+
+    lax.fori_loop(0, CELLS, tables, 0)
 
     pl.semaphore_wait(barrier, BLOCKS - 1 + 2 * (SIDE - 1) + 2)
 
-    def exchange(k, sent, received, ssem, rsem):
+    def exchange(sent, received, ssem, rsem, *at):
         return [
             copy(
-                sent.at[k, side], received.at[k, 1 - side],
-                ssem.at[k, side], rsem.at[k, 1 - side], slab=neighbour[side],
+                sent.at[(*at, side)], received.at[(*at, 1 - side)],
+                ssem.at[(*at, side)], rsem.at[(*at, 1 - side)], slab=neighbour[side],
             )
             for side in range(2)
         ]
@@ -225,26 +280,34 @@
         for side in range(2):
             pl.when(has[side])(copies[side].wait_send)
 
-    groups = [slice(g * PACK, (g + 1) * PACK) for g in range(ROWS // PACK)]
-    local_tiles, side_tiles, own_tiles = LOCAL // LANES, FACE // LANES, OWN // LANES
+    first = exchange(first_out, first_in, first_ssem, first_rsem)
+    start_both(first)
+
     nothing = jnp.zeros((PACK, LANES), BF16)
 
-    def span(t, width=LANES):
-        return slice(t * width, (t + 1) * width)
-
-    def side_of(buffer, k, t, g):
-        return buffer[k, t // side_tiles, groups[g], span(t % side_tiles)]
-
-    def send_faces(k):
-        for j in range(2 * side_tiles):
-            for rows in groups:
-                halo_out[k, j // side_tiles, rows, span(j % side_tiles)] = pick_among(
-                    [(t, rounded[rows, span(t)]) for t in range(own_tiles)],
-                    face_from[j, 0], face_from[j, 1], nothing,
-                )
-        copies = exchange(k, halo_out, halo, halo_ssem, halo_rsem)
-        start_both(copies)
-        return copies
+    def gather_own(i, _):
+        for c in (2 * i, 2 * i + 1):
+            for j in range(local_tiles):
+                for rows in groups:
+                    pieces[c, rows, span(j)] = pick_among(
+                        [(t, rounded[rows, span(t)]) for t in range(OWN_TILES)],
+                        gather_at[c, j, 0], gather_at[c, j, 1], nothing,
+                    )
+        return 0
+
+    def multiply(i, _):
+        for c in (2 * i, 2 * i + 1):
+            for j in range(local_tiles):
+                for rows in groups:
+                    pieces[c, rows, span(j)] = pick_among(
+                        [
+                            (OWN_TILES + t, rounded_border[rows, span(t)])
+                            for t in range(BORDER_TILES)
+                        ],
+                        gather_at[c, j, 0], gather_at[c, j, 1], pieces[c, rows, span(j)],
+                    )
+            terms[c] = jnp.dot(pieces[c], matrices[c], preferred_element_type=F32).astype(BF16)
+        return 0
 
     def gathered(t, g):
         total = jnp.zeros((PACK, LANES), F32)
@@ -255,88 +318,69 @@
             ).astype(F32)
         return total
 
-    fields = [field_a, field_b]
+    def scatter_border(i, _):
+        for t in range(STEP_TILES):
+            t = STEP_TILES * i + t
+            columns = pl.ds(pl.multiple_of(t * LANES, LANES), LANES)
+            for g, rows in enumerate(groups):
+                part[rows, columns] = gathered(OWN_TILES + t, g)
+        return 0
+
+    lax.fori_loop(0, CELLS // 2, gather_own, 0)
+    load.wait()
+    land_both(first)
+    for side in range(2):
+        border_a[:, span(2 + side, FACE)] = first_in[side]
+    rounded_border[...] = border_a[...].astype(BF16)
+    leave_both(first)
+
+    fields, borders = [field_a, field_b], [border_a, border_b]
     for k in range(DEGREE):
-        halo_copies = send_faces(k)
-        if k == 0:
-
-            def tables(c, _):
-                wanted = connectivity[pl.ds(c, 1), :]
-                split_tables(wanted, gather_at.at[c])
-                inverse_tables(wanted, EXT_TILES, scatter_at.at[c])
-                return 0
-
-            lax.fori_loop(0, CELLS, tables, 0)
-
-        def gather_own(i, _):
-            for c in (2 * i, 2 * i + 1):
-                for j in range(local_tiles):
-                    for rows in groups:
-                        pieces[c, rows, span(j)] = pick_among(
-                            [(t + side_tiles, rounded[rows, span(t)]) for t in range(own_tiles)],
-                            gather_at[c, j, 0], gather_at[c, j, 1], nothing,
-                        )
-            return 0
-
-        lax.fori_loop(0, CELLS // 2, gather_own, 0)
-        if k == 0:
-            load.wait()
-        land_both(halo_copies)
-
-        def cell(i, _):
-            for c in (2 * i, 2 * i + 1):
-                for j in range(local_tiles):
-                    for g, rows in enumerate(groups):
-                        pieces[c, rows, span(j)] = pick_among(
-                            [
-                                (t if t < side_tiles else t + own_tiles, side_of(halo, k, t, g))
-                                for t in range(2 * side_tiles)
-                            ],
-                            gather_at[c, j, 0], gather_at[c, j, 1], pieces[c, rows, span(j)],
-                        )
-                terms[c] = jnp.dot(
-                    pieces[c], matrices[c], preferred_element_type=F32
-                ).astype(BF16)
-            return 0
-
-        lax.fori_loop(0, CELLS // 2, cell, 0)
-        for t in range(2 * side_tiles):
-            for g, rows in enumerate(groups):
-                back_out[k, t // side_tiles, rows, span(t % side_tiles)] = gathered(
-                    t if t < side_tiles else t + own_tiles, g
-                ).astype(BF16)
-        back_copies = exchange(k, back_out, back, back_ssem, back_rsem)
-        start_both(back_copies)
-
-        target = fields[(k + 1) % 2]
+        lax.fori_loop(0, CELLS // 2, multiply, 0)
+        lax.fori_loop(0, BORDER_TILES // STEP_TILES, scatter_border, 0)
+        for side in range(2):
+            shared_out[k, side, 0] = part[:, span(2 + side, FACE)].astype(BF16)
+            shared_out[k, side, 1] = part[:, span(side, FACE)].astype(BF16)
+        copies = exchange(shared_out, shared_in, shared_ssem, shared_rsem, k)
+        start_both(copies)
+
+        target, target_border = fields[(k + 1) % 2], borders[(k + 1) % 2]
 
         def scatter_own(i, _):
-            for t in (2 * i, 2 * i + 1):
+            for t in range(STEP_TILES):
+                t = STEP_TILES * i + t
                 columns = pl.ds(pl.multiple_of(t * LANES, LANES), LANES)
                 for g, rows in enumerate(groups):
-                    total = gathered(t + side_tiles, g)
+                    total = gathered(t, g)
                     if k > 0:
                         total = 2.0 * total - target[rows, columns]
                     target[rows, columns] = total
+                    rounded[rows, columns] = total.astype(BF16)
             return 0
 
-        lax.fori_loop(0, own_tiles // 2, scatter_own, 0)
-        land_both(back_copies)
-        for t in range(own_tiles):
-            for g, rows in enumerate(groups):
-                added = pick_among(
-                    [(h, side_of(back, k, h, g)) for h in range(2 * side_tiles)],
-                    face_to[t, 0], face_to[t, 1], nothing,
-                ).astype(F32)
-                current = target[rows, span(t)] + (added if k == 0 else 2.0 * added)
-                if k < DEGREE - 1:
-                    target[rows, span(t)] = current
-                    rounded[rows, span(t)] = current.astype(BF16)
-                else:
-                    p, q = divmod(t, PIECE // LANES)
-                    blocks[o, p, rows, span(q)] = current.astype(BF16)
-        leave_both(halo_copies)
-        leave_both(back_copies)
+        lax.fori_loop(0, OWN_TILES // STEP_TILES, scatter_own, 0)
+        if k < DEGREE - 1:
+            lax.fori_loop(0, CELLS // 2, gather_own, 0)
+        land_both(copies)
+        for side in range(2):
+            present = jnp.where(has[side], 1.0, 0.0)
+            for kind, columns in enumerate((span(side, FACE), span(2 + side, FACE))):
+                total = part[:, columns] + shared_in[k, side, kind].astype(F32)
+                if kind == 1:
+                    total = total * present
+                if k > 0:
+                    total = 2.0 * total - target_border[:, columns]
+                target_border[:, columns] = total
+                rounded_border[:, columns] = total.astype(BF16)
+        leave_both(copies)
+
+    for t in range(OWN_TILES):
+        p, q = divmod(t, PIECE // LANES)
+        for rows in groups:
+            blocks[o, p, rows, span(q)] = pick_among(
+                [(h, rounded_border[rows, span(h)]) for h in range(2 * side_tiles)],
+                face_to[t, 0], face_to[t, 1], rounded[rows, span(t)],
+            )
 
     def turn(at):
         return lax.rem(at + BLOCKS, BLOCKS)
@@ -441,29 +485,32 @@
 
 
 def per_device(orbitals, cell_matrices, connectivity, face_lower, face_upper):
-    faces = jnp.concatenate([face_lower, face_upper], axis=0)[None, :]
     vmem = pl.BlockSpec(memory_space=pltpu.VMEM)
     dma = pltpu.SemaphoreType.DMA
     return pl.pallas_call(
         kernel,
         out_shape=jax.ShapeDtypeStruct((ROWS, OWN), F32),
-        in_specs=[vmem, vmem, vmem, pl.BlockSpec(memory_space=pl.ANY)],
+        in_specs=[vmem, vmem, vmem, vmem, pl.BlockSpec(memory_space=pl.ANY)],
         out_specs=vmem,
         scratch_shapes=[
+            pltpu.VMEM((CELLS, LOCAL), jnp.int32),
             pltpu.VMEM((CELLS, LOCAL // LANES, 2, PACK, LANES), jnp.int16),
-            pltpu.VMEM((CELLS, EXT_TILES, 2, PACK, LANES), jnp.int16),
-            pltpu.VMEM((LOCAL // LANES, 2, PACK, LANES), jnp.int16),
-            pltpu.VMEM((OWN // LANES, 2, PACK, LANES), jnp.int16),
+            pltpu.VMEM((CELLS, TILES, 2, PACK, LANES), jnp.int16),
+            pltpu.VMEM((OWN_TILES, 2, PACK, LANES), jnp.int16),
             pltpu.VMEM((CELLS, LOCAL, LOCAL), BF16),
             pltpu.VMEM((ROWS, OWN), F32),
             pltpu.VMEM((ROWS, OWN), F32),
+            pltpu.VMEM((ROWS, BORDER), F32),
+            pltpu.VMEM((ROWS, BORDER), F32),
+            pltpu.VMEM((ROWS, BORDER), F32),
             pltpu.VMEM((ROWS, OWN), BF16),
+            pltpu.VMEM((ROWS, BORDER), BF16),
             pltpu.VMEM((CELLS, ROWS, LOCAL), BF16),
             pltpu.VMEM((CELLS, ROWS, LOCAL), BF16),
-            pltpu.VMEM((DEGREE, 2, ROWS, FACE), BF16),
-            pltpu.VMEM((DEGREE, 2, ROWS, FACE), BF16),
-            pltpu.VMEM((DEGREE, 2, ROWS, FACE), BF16),
-            pltpu.VMEM((DEGREE, 2, ROWS, FACE), BF16),
+            pltpu.VMEM((2, ROWS, FACE), F32),
+            pltpu.VMEM((2, ROWS, FACE), F32),
+            pltpu.VMEM((DEGREE, 2, 2, ROWS, FACE), BF16),
+            pltpu.VMEM((DEGREE, 2, 2, ROWS, FACE), BF16),
             pltpu.VMEM((BLOCKS, PIECES, ROWS, PIECE), BF16),
             pltpu.VMEM((2, HALF, ALL), F32),
             pltpu.VMEM((HALF, ALL), F32),
@@ -473,7 +520,7 @@
             pltpu.VMEM((ALL, ALL), F32),
             pltpu.VMEM((BLOCKS, ROWS, ALL), F32),
             dma,
-            dma((DEGREE, 2)), dma((DEGREE, 2)), dma((DEGREE, 2)), dma((DEGREE, 2)),
+            dma((2,)), dma((2,)), dma((DEGREE, 2)), dma((DEGREE, 2)),
             dma((2, BLOCKS // 2, PIECES)), dma((2, BLOCKS // 2, PIECES)),
             dma, dma,
             dma((SIDE,)), dma((SIDE,)), dma((SIDE,)), dma((SIDE,)),
@@ -481,7 +528,7 @@
         ],
         compiler_params=pltpu.CompilerParams(collective_id=0, has_side_effects=True),
         name="filter_and_orthonormalize",
-    )(orbitals, connectivity, faces, cell_matrices)
+    )(orbitals, connectivity, face_lower[None, :], face_upper[None, :], cell_matrices)
 
 
 def solution(mesh):

time: 89.5 us -> 83.2 us (0.930)
  Pallas kernels: 86.4 us -> 81.4 us
  other arithmetic: 1.28 us -> 0 us
    pallas_call x1, Pallas kernels: 86.4 us -> 81.4 us  [per_device(): pl.pallas_call(kernel, out_shape=jax.ShapeDtypeStruct((ROWS, OWN), F32),...]
    concatenate x1 -> x0, other arithmetic: 1.28 us -> none  [per_device(): faces = jnp.concatenate([face_lower, face_upper], axis=0)[None, :]]
where the time goes in v3:
time: 83.2 us; the launch traced here: 83.1 us
  Pallas kernels  81.4 us (98%)
  local copies, waits for them, and re-layouts  1.67 us (2%)
    pallas_call x1, Pallas kernels, per_device(): pl.pallas_call(kernel, out_shape=jax.ShapeDtypeStruct((ROWS, OWN), F32),...  81.4 us
    unnamed x1, local copies, waits for them, and re-layouts  1.67 us

profile of v3, /device:TPU:1, one launch (start us, length us, event | category | flops | bytes accessed | tf_op | source)
XLA Modules:
  0.0 83.1 jit_solution(10170621530634621884)
XLA Ops:
  0.0 81.4 %filter_and_orthonormalize.1 = f32[32,2048]{1,0:T(8,128)} custom-call(f32[32,2048]{1,0:T(8,128)} %orbitals.1, s32[8,512]{1,0:T(8,128)} %connectivity.1, s32[1,256]{1,0:T(1,128)} %bitcast.2, s32[1,256]{1,0:T(1,128)} %bitcast.3, bf16[8,512,512]{2,1,0:T(8,128)(2,1)} %matrices_hbm.1), custom_call_target="tpu_custom_call" | custom-call | tf_op jit(solution)/shard_map/filter_and_orthonormalize/pallas_call | solution.py:490
  81.4 1.7 %copy.7 = f32[32,2048]{1,0:T(8,128)} copy(f32[32,2048]{1,0:T(8,128)} %filter_and_orthonormalize.1) | data formatting | bytes 524288

commit v4 on v3

--- a/solution.py
+++ b/solution.py
@@ -33,6 +33,7 @@
 PIECES = 4
 PIECE = OWN // PIECES
 HALF = ROWS // 2
+SHARED = (ROWS + HALF) // 2
 ALL = ROWS * BLOCKS
 
 
@@ -295,35 +296,45 @@
                     )
         return 0
 
-    def multiply(i, _):
+    def multiply(i):
         for c in (2 * i, 2 * i + 1):
-            for j in range(local_tiles):
-                for rows in groups:
-                    pieces[c, rows, span(j)] = pick_among(
-                        [
-                            (OWN_TILES + t, rounded_border[rows, span(t)])
-                            for t in range(BORDER_TILES)
-                        ],
-                        gather_at[c, j, 0], gather_at[c, j, 1], pieces[c, rows, span(j)],
-                    )
-            terms[c] = jnp.dot(pieces[c], matrices[c], preferred_element_type=F32).astype(BF16)
-        return 0
-
-    def gathered(t, g):
+            parts = [
+                jnp.concatenate(
+                    [
+                        pick_among(
+                            [
+                                (OWN_TILES + t, rounded_border[rows, span(t)])
+                                for t in range(BORDER_TILES)
+                            ],
+                            gather_at[c, j, 0], gather_at[c, j, 1], pieces[c, rows, span(j)],
+                        )
+                        for rows in groups
+                    ],
+                    axis=0,
+                )
+                for j in range(local_tiles)
+            ]
+            terms[c] = jnp.dot(
+                jnp.concatenate(parts, axis=1), matrices[c], preferred_element_type=F32
+            ).astype(BF16)
+
+    def gathered(t, g, cells):
         total = jnp.zeros((PACK, LANES), F32)
-        for c in range(CELLS):
+        for c in cells:
             total += pick_among(
                 [(h, terms[c, groups[g], span(h)]) for h in range(local_tiles)],
                 scatter_at[c, t, 0], scatter_at[c, t, 1], nothing,
             ).astype(F32)
         return total
 
-    def scatter_border(i, _):
-        for t in range(STEP_TILES):
-            t = STEP_TILES * i + t
-            columns = pl.ds(pl.multiple_of(t * LANES, LANES), LANES)
+    def add_border(i):
+        for t in range(BORDER_TILES):
             for g, rows in enumerate(groups):
-                part[rows, columns] = gathered(OWN_TILES + t, g)
+                part[rows, span(t)] += gathered(OWN_TILES + t, g, (2 * i, 2 * i + 1))
+
+    def multiply_and_add(i, _):
+        add_border(i - 1)
+        multiply(i)
         return 0
 
     lax.fori_loop(0, CELLS // 2, gather_own, 0)
@@ -336,8 +347,10 @@
 
     fields, borders = [field_a, field_b], [border_a, border_b]
     for k in range(DEGREE):
-        lax.fori_loop(0, CELLS // 2, multiply, 0)
-        lax.fori_loop(0, BORDER_TILES // STEP_TILES, scatter_border, 0)
+        part[...] = jnp.zeros_like(part)
+        multiply(0)
+        lax.fori_loop(1, CELLS // 2, multiply_and_add, 0)
+        add_border(CELLS // 2 - 1)
         for side in range(2):
             shared_out[k, side, 0] = part[:, span(2 + side, FACE)].astype(BF16)
             shared_out[k, side, 1] = part[:, span(side, FACE)].astype(BF16)
@@ -351,7 +364,7 @@
                 t = STEP_TILES * i + t
                 columns = pl.ds(pl.multiple_of(t * LANES, LANES), LANES)
                 for g, rows in enumerate(groups):
-                    total = gathered(t, g)
+                    total = gathered(t, g, range(CELLS))
                     if k > 0:
                         total = 2.0 * total - target[rows, columns]
                     target[rows, columns] = total
@@ -400,7 +413,8 @@
         )
 
     sent = []
-    for d in range(1, far + 2):
+
+    def relay(d):
         for p in range(PIECES):
             for way in range(2):
                 if d > 1 and moves(way, d - 1, p):
@@ -410,13 +424,30 @@
                     one.start()
                     sent.append(one)
 
-    strip = jnp.zeros((ROWS, ALL), F32)
+    for d in range(1, far):
+        relay(d)
+
+    quarter, share = lax.rem(o + 2, far), turn(o - 2) // far
+    products = jnp.zeros((2 * ROWS + HALF, 5 * ROWS), F32)
     for p in range(PIECES):
-        strip += lax.dot_general(
-            blocks[o, p], blocks[:, p].reshape(ALL, PIECE), NT, preferred_element_type=F32
-        )
-    halves[0] = strip[:HALF]
-    halves[1] = strip[HALF:]
+        left = jnp.concatenate(
+            [
+                blocks[o, p], blocks[turn(o - 1), p],
+                blocks[quarter, p, pl.ds(pl.multiple_of(share * HALF, HALF), HALF), :],
+            ],
+            axis=0,
+        )
+        right = jnp.concatenate(
+            [blocks[turn(o + k), p] for k in (0, 1, 2, 1)] + [blocks[quarter + far, p]], axis=0
+        )
+        products += lax.dot_general(left, right, NT, preferred_element_type=F32)
+    near = lax.broadcasted_iota(jnp.int32, (ROWS, LANES), 1) < 2 * ROWS
+    strip = jnp.where(near, products[:ROWS, :LANES], products[ROWS : 2 * ROWS, :LANES])
+    halves[0] = strip[:SHARED]
+    halves[1, : ROWS - SHARED] = strip[SHARED:]
+    halves[1, ROWS - SHARED :] = jnp.concatenate(
+        [products[2 * ROWS :, LANES:], jnp.zeros((HALF, LANES - ROWS), F32)], axis=1
+    )
 
     one = copy(halves.at[1 - core], half_in, core_ssem, core_rsem, slab=other_core)
     one.start()
@@ -434,6 +465,7 @@
     for one in copies:
         one.wait()
     along_y[0] = (along_x[0] + along_x[1]) + (along_x[2] + along_x[3])
+    relay(far)
     copies = [
         copy(
             along_y.at[0], along_y.at[d], y_ssem.at[d], y_rsem.at[d],
@@ -466,13 +498,29 @@
         pair(turn(o - d)).start()
     for k in range(BLOCKS):
         pair(k).wait()
+    relay(far + 1)
     for one in copies + sent:
         one.wait_send()
 
-    for k in range(BLOCKS):
-        for h in range(2):
-            first = k * ROWS + h * HALF
-            gram[first : first + HALF, :] = rows_all[h, k]
+    strips = [
+        jnp.concatenate([rows_all[0, k], rows_all[1, k, : ROWS - SHARED]], axis=0)
+        for k in range(BLOCKS)
+    ]
+    strips = [jnp.where(near, strips[k], strips[(k + 1) % BLOCKS]) for k in range(BLOCKS)]
+    place = (0, 1, 3, 2)
+    for i in range(BLOCKS):
+        rows = span(i, ROWS)
+        for j in range(i, BLOCKS):
+            away = j - i
+            if away < far:
+                gram[rows, span(j, ROWS)] = strips[i][:, span(place[away], ROWS)]
+            elif away > far:
+                gram[rows, span(j, ROWS)] = strips[j][:, span(place[BLOCKS - away], ROWS)].T
+            else:
+                for half in range(2):
+                    gram[i * ROWS + half * HALF : i * ROWS + (half + 1) * HALF, span(j, ROWS)] = (
+                        rows_all[1, (i + 2 + half * far) % BLOCKS, ROWS - SHARED :, :ROWS]
+                    )
     invert_factor(gram, inverse)
 
     weights = inverse[o] * math.sqrt(OWN * SLABS)
@@ -512,11 +560,11 @@
             pltpu.VMEM((DEGREE, 2, 2, ROWS, FACE), BF16),
             pltpu.VMEM((DEGREE, 2, 2, ROWS, FACE), BF16),
             pltpu.VMEM((BLOCKS, PIECES, ROWS, PIECE), BF16),
-            pltpu.VMEM((2, HALF, ALL), F32),
-            pltpu.VMEM((HALF, ALL), F32),
-            pltpu.VMEM((SIDE, HALF, ALL), F32),
-            pltpu.VMEM((SIDE, HALF, ALL), F32),
-            pltpu.VMEM((2, BLOCKS, HALF, ALL), F32),
+            pltpu.VMEM((2, SHARED, LANES), F32),
+            pltpu.VMEM((SHARED, LANES), F32),
+            pltpu.VMEM((SIDE, SHARED, LANES), F32),
+            pltpu.VMEM((SIDE, SHARED, LANES), F32),
+            pltpu.VMEM((2, BLOCKS, SHARED, LANES), F32),
             pltpu.VMEM((ALL, ALL), F32),
             pltpu.VMEM((BLOCKS, ROWS, ALL), F32),
             dma,

time: 83.2 us -> 75.5 us (0.907)
  Pallas kernels: 81.4 us -> 73.7 us
    pallas_call x1, Pallas kernels: 81.4 us -> 73.7 us  [per_device(): pl.pallas_call(kernel, out_shape=jax.ShapeDtypeStruct((ROWS, OWN), F32),...]
where the time goes in v4:
time: 75.5 us; the launch traced here: 75.3 us
  Pallas kernels  73.7 us (98%)
  local copies, waits for them, and re-layouts  1.67 us (2%)
    pallas_call x1, Pallas kernels, per_device(): pl.pallas_call(kernel, out_shape=jax.ShapeDtypeStruct((ROWS, OWN), F32),...  73.7 us
    unnamed x1, local copies, waits for them, and re-layouts  1.67 us

profile of v4, /device:TPU:1, one launch (start us, length us, event | category | flops | bytes accessed | tf_op | source)
XLA Modules:
  0.0 75.3 jit_solution(11146677364969456699)
XLA Ops:
  0.0 73.7 %filter_and_orthonormalize.1 = f32[32,2048]{1,0:T(8,128)} custom-call(f32[32,2048]{1,0:T(8,128)} %orbitals.1, s32[8,512]{1,0:T(8,128)} %connectivity.1, s32[1,256]{1,0:T(1,128)} %bitcast.2, s32[1,256]{1,0:T(1,128)} %bitcast.3, bf16[8,512,512]{2,1,0:T(8,128)(2,1)} %matrices_hbm.1), custom_call_target="tpu_custom_call" | custom-call | tf_op jit(solution)/shard_map/filter_and_orthonormalize/pallas_call | solution.py:538
  73.7 1.7 %copy.7 = f32[32,2048]{1,0:T(8,128)} copy(f32[32,2048]{1,0:T(8,128)} %filter_and_orthonormalize.1) | data formatting | bytes 524288

commit v5 on v4

--- a/solution.py
+++ b/solution.py
@@ -169,7 +169,8 @@
 
 
 def kernel(
-    orbitals, connectivity, lower, upper, matrices_hbm, out,
+    orbitals_hbm, connectivity_hbm, lower_hbm, upper_hbm, matrices_hbm, out,
+    orbitals, connectivity, lower, upper,
     places, gather_at, scatter_at, face_to, matrices, field_a, field_b, border_a, border_b,
     part, rounded, rounded_border, pieces, terms,
     first_out, first_in, shared_out, shared_in,
@@ -194,6 +195,17 @@
     has = (s > 0, s < SLABS - 1)
     neighbour = (down, up)
 
+    inputs = [
+        pltpu.make_async_copy(source, held, load_sem.at[n])
+        for n, (source, held) in enumerate(
+            [
+                (lower_hbm, lower), (upper_hbm, upper),
+                (orbitals_hbm, orbitals), (connectivity_hbm, connectivity),
+            ]
+        )
+    ]
+    for one in inputs:
+        one.start()
     first_in[...] = jnp.zeros_like(first_in)
     shared_in[...] = jnp.zeros_like(shared_in)
 
@@ -211,7 +223,9 @@
     for there in neighbour:
         pl.semaphore_signal(barrier, inc=1, device_id={"slab": there}, device_id_type=MESH)
 
-    load = pltpu.make_async_copy(matrices_hbm, matrices, load_sem)
+    for one in inputs:
+        one.wait()
+    load = pltpu.make_async_copy(matrices_hbm, matrices, load_sem.at[4])
     load.start()
 
     groups = [slice(g * PACK, (g + 1) * PACK) for g in range(ROWS // PACK)]
@@ -296,27 +310,27 @@
                     )
         return 0
 
-    def multiply(i):
+    def complete(i):
         for c in (2 * i, 2 * i + 1):
-            parts = [
-                jnp.concatenate(
-                    [
-                        pick_among(
-                            [
-                                (OWN_TILES + t, rounded_border[rows, span(t)])
-                                for t in range(BORDER_TILES)
-                            ],
-                            gather_at[c, j, 0], gather_at[c, j, 1], pieces[c, rows, span(j)],
-                        )
-                        for rows in groups
-                    ],
-                    axis=0,
-                )
-                for j in range(local_tiles)
-            ]
-            terms[c] = jnp.dot(
-                jnp.concatenate(parts, axis=1), matrices[c], preferred_element_type=F32
-            ).astype(BF16)
+            for j in range(local_tiles):
+                for rows in groups:
+                    pieces[c, rows, span(j)] = pick_among(
+                        [
+                            (OWN_TILES + t, rounded_border[rows, span(t)])
+                            for t in range(BORDER_TILES)
+                        ],
+                        gather_at[c, j, 0], gather_at[c, j, 1], pieces[c, rows, span(j)],
+                    )
+
+    def products_of(i):
+        return [
+            jnp.dot(pieces[c], matrices[c], preferred_element_type=F32).astype(BF16)
+            for c in (2 * i, 2 * i + 1)
+        ]
+
+    def keep(i, products):
+        for c, product in enumerate(products):
+            terms[2 * i + c] = product
 
     def gathered(t, g, cells):
         total = jnp.zeros((PACK, LANES), F32)
@@ -332,9 +346,11 @@
             for g, rows in enumerate(groups):
                 part[rows, span(t)] += gathered(OWN_TILES + t, g, (2 * i, 2 * i + 1))
 
-    def multiply_and_add(i, _):
+    def middle(i, _):
+        products = products_of(i)
         add_border(i - 1)
-        multiply(i)
+        complete(i + 1)
+        keep(i, products)
         return 0
 
     lax.fori_loop(0, CELLS // 2, gather_own, 0)
@@ -348,8 +364,14 @@
     fields, borders = [field_a, field_b], [border_a, border_b]
     for k in range(DEGREE):
         part[...] = jnp.zeros_like(part)
-        multiply(0)
-        lax.fori_loop(1, CELLS // 2, multiply_and_add, 0)
+        complete(0)
+        products = products_of(0)
+        complete(1)
+        keep(0, products)
+        lax.fori_loop(1, CELLS // 2 - 1, middle, 0)
+        products = products_of(CELLS // 2 - 1)
+        add_border(CELLS // 2 - 2)
+        keep(CELLS // 2 - 1, products)
         add_border(CELLS // 2 - 1)
         for side in range(2):
             shared_out[k, side, 0] = part[:, span(2 + side, FACE)].astype(BF16)
@@ -414,7 +436,7 @@
 
     sent = []
 
-    def relay(d):
+    def relay(d, arrived=lambda p: None):
         for p in range(PIECES):
             for way in range(2):
                 if d > 1 and moves(way, d - 1, p):
@@ -423,13 +445,12 @@
                     one = ring(way, d, p)
                     one.start()
                     sent.append(one)
-
-    for d in range(1, far):
-        relay(d)
+            arrived(p)
 
     quarter, share = lax.rem(o + 2, far), turn(o - 2) // far
-    products = jnp.zeros((2 * ROWS + HALF, 5 * ROWS), F32)
-    for p in range(PIECES):
+    sums = []
+
+    def multiply_blocks(p):
         left = jnp.concatenate(
             [
                 blocks[o, p], blocks[turn(o - 1), p],
@@ -440,7 +461,12 @@
         right = jnp.concatenate(
             [blocks[turn(o + k), p] for k in (0, 1, 2, 1)] + [blocks[quarter + far, p]], axis=0
         )
-        products += lax.dot_general(left, right, NT, preferred_element_type=F32)
+        sums.append(lax.dot_general(left, right, NT, preferred_element_type=F32))
+
+    relay(1)
+    relay(2)
+    relay(3, multiply_blocks)
+    products = (sums[0] + sums[1]) + (sums[2] + sums[3])
     near = lax.broadcasted_iota(jnp.int32, (ROWS, LANES), 1) < 2 * ROWS
     strip = jnp.where(near, products[:ROWS, :LANES], products[ROWS : 2 * ROWS, :LANES])
     halves[0] = strip[:SHARED]
@@ -538,9 +564,13 @@
     return pl.pallas_call(
         kernel,
         out_shape=jax.ShapeDtypeStruct((ROWS, OWN), F32),
-        in_specs=[vmem, vmem, vmem, vmem, pl.BlockSpec(memory_space=pl.ANY)],
+        in_specs=[pl.BlockSpec(memory_space=pl.ANY)] * 5,
         out_specs=vmem,
         scratch_shapes=[
+            pltpu.VMEM((ROWS, OWN), F32),
+            pltpu.VMEM((CELLS, LOCAL), jnp.int32),
+            pltpu.VMEM((1, FACE), jnp.int32),
+            pltpu.VMEM((1, FACE), jnp.int32),
             pltpu.VMEM((CELLS, LOCAL), jnp.int32),
             pltpu.VMEM((CELLS, LOCAL // LANES, 2, PACK, LANES), jnp.int16),
             pltpu.VMEM((CELLS, TILES, 2, PACK, LANES), jnp.int16),
@@ -567,7 +597,7 @@
             pltpu.VMEM((2, BLOCKS, SHARED, LANES), F32),
             pltpu.VMEM((ALL, ALL), F32),
             pltpu.VMEM((BLOCKS, ROWS, ALL), F32),
-            dma,
+            dma((5,)),
             dma((2,)), dma((2,)), dma((DEGREE, 2)), dma((DEGREE, 2)),
             dma((2, BLOCKS // 2, PIECES)), dma((2, BLOCKS // 2, PIECES)),
             dma, dma,

time: 75.5 us -> 71.8 us (0.951)
  Pallas kernels: 73.7 us -> 70 us
    pallas_call x1, Pallas kernels: 73.7 us -> 70 us  [per_device(): pl.pallas_call(kernel, out_shape=jax.ShapeDtypeStruct((ROWS, OWN), F32),...]
where the time goes in v5:
time: 71.8 us; the launch traced here: 71.7 us
  Pallas kernels  70 us (97%)
  local copies, waits for them, and re-layouts  1.67 us (2%)
    pallas_call x1, Pallas kernels, per_device(): pl.pallas_call(kernel, out_shape=jax.ShapeDtypeStruct((ROWS, OWN), F32),...  70 us
    unnamed x1, local copies, waits for them, and re-layouts  1.67 us

profile of v5, /device:TPU:1, one launch (start us, length us, event | category | flops | bytes accessed | tf_op | source)
XLA Modules:
  0.0 71.7 jit_solution(13923968985360317819)
XLA Ops:
  0.0 70.0 %filter_and_orthonormalize.1 = f32[32,2048]{1,0:T(8,128)} custom-call(f32[32,2048]{1,0:T(8,128)} %orbitals_hbm.1, s32[8,512]{1,0:T(8,128)} %connectivity_hbm.1, s32[1,256]{1,0:T(1,128)} %bitcast.2, s32[1,256]{1,0:T(1,128)} %bitcast.3, bf16[8,512,512]{2,1,0:T(8,128)(2,1)} %matrices_hbm.1), custom_call_target="tpu_custom_call" | custom-call | tf_op jit(solution)/shard_map/filter_and_orthonormalize/pallas_call | solution.py:564
  70.0 1.7 %copy.7 = f32[32,2048]{1,0:T(8,128)} copy(f32[32,2048]{1,0:T(8,128)} %filter_and_orthonormalize.1) | data formatting | bytes 524288

commit v6 on v5

--- a/solution.py
+++ b/solution.py
@@ -29,7 +29,9 @@
 BLOCKS = 8
 SLABS = 32
 SIDE = 4
-STEP_TILES = 4
+DENSE = 4
+SPARSE = OWN // LANES - DENSE
+STEPS = 4
 PIECES = 4
 PIECE = OWN // PIECES
 HALF = ROWS // 2
@@ -171,7 +173,7 @@
 def kernel(
     orbitals_hbm, connectivity_hbm, lower_hbm, upper_hbm, matrices_hbm, out,
     orbitals, connectivity, lower, upper,
-    places, gather_at, scatter_at, face_to, matrices, field_a, field_b, border_a, border_b,
+    places, gather_at, scatter_at, face_to, picker, dense, matrices, field_a, field_b, border_a, border_b,
     part, rounded, rounded_border, pieces, terms,
     first_out, first_in, shared_out, shared_in,
     blocks, halves, half_in, along_x, along_y, rows_all, gram, inverse,
@@ -298,16 +300,28 @@
     first = exchange(first_out, first_in, first_ssem, first_rsem)
     start_both(first)
 
+    def pick_dense(c, _):
+        first_row = SPARSE * LANES
+        wanted = places[pl.ds(c, 1), :] - first_row
+        numbers = lax.broadcasted_iota(jnp.int32, (DENSE * LANES, LOCAL), 0)
+        picker[c] = jnp.where(numbers == wanted, 1.0, 0.0).astype(BF16)
+        return 0
+
+    lax.fori_loop(0, CELLS, pick_dense, 0)
+
     nothing = jnp.zeros((PACK, LANES), BF16)
 
     def gather_own(i, _):
         for c in (2 * i, 2 * i + 1):
+            exact = jnp.dot(
+                rounded[:, SPARSE * LANES :], picker[c], preferred_element_type=F32
+            ).astype(BF16)
             for j in range(local_tiles):
                 for rows in groups:
                     pieces[c, rows, span(j)] = pick_among(
-                        [(t, rounded[rows, span(t)]) for t in range(OWN_TILES)],
+                        [(t, rounded[rows, span(t)]) for t in range(SPARSE)],
                         gather_at[c, j, 0], gather_at[c, j, 1], nothing,
-                    )
+                    ) + exact[rows, span(j)]
         return 0
 
     def complete(i):
@@ -381,19 +395,26 @@
 
         target, target_border = fields[(k + 1) % 2], borders[(k + 1) % 2]
 
-        def scatter_own(i, _):
-            for t in range(STEP_TILES):
-                t = STEP_TILES * i + t
+        def advance(rows, columns, total):
+            if k > 0:
+                total = 2.0 * total - target[rows, columns]
+            target[rows, columns] = total
+            rounded[rows, columns] = total.astype(BF16)
+
+        def scatter_own(i, total):
+            for c in (2 * i, 2 * i + 1):
+                total += lax.dot_general(terms[c], picker[c], NT, preferred_element_type=F32)
+            for t in range(SPARSE // STEPS):
+                t = SPARSE // STEPS * i + t
                 columns = pl.ds(pl.multiple_of(t * LANES, LANES), LANES)
                 for g, rows in enumerate(groups):
-                    total = gathered(t, g, range(CELLS))
-                    if k > 0:
-                        total = 2.0 * total - target[rows, columns]
-                    target[rows, columns] = total
-                    rounded[rows, columns] = total.astype(BF16)
-            return 0
-
-        lax.fori_loop(0, OWN_TILES // STEP_TILES, scatter_own, 0)
+                    advance(rows, columns, gathered(t, g, range(CELLS)))
+            return total
+
+        dense[...] = lax.fori_loop(
+            0, STEPS, scatter_own, jnp.zeros((ROWS, DENSE * LANES), F32)
+        )
+        advance(slice(None), slice(SPARSE * LANES, OWN), dense[...])
         if k < DEGREE - 1:
             lax.fori_loop(0, CELLS // 2, gather_own, 0)
         land_both(copies)
@@ -575,6 +596,8 @@
             pltpu.VMEM((CELLS, LOCAL // LANES, 2, PACK, LANES), jnp.int16),
             pltpu.VMEM((CELLS, TILES, 2, PACK, LANES), jnp.int16),
             pltpu.VMEM((OWN_TILES, 2, PACK, LANES), jnp.int16),
+            pltpu.VMEM((CELLS, DENSE * LANES, LOCAL), BF16),
+            pltpu.VMEM((ROWS, DENSE * LANES), F32),
             pltpu.VMEM((CELLS, LOCAL, LOCAL), BF16),
             pltpu.VMEM((ROWS, OWN), F32),
             pltpu.VMEM((ROWS, OWN), F32),

time: 71.8 us -> 70.9 us (0.987)
  Pallas kernels: 70 us -> 69.1 us
    pallas_call x1, Pallas kernels: 70 us -> 69.1 us  [per_device(): pl.pallas_call(kernel, out_shape=jax.ShapeDtypeStruct((ROWS, OWN), F32),...]
where the time goes in v6:
time: 70.9 us; the launch traced here: 70.7 us
  Pallas kernels  69.1 us (97%)
  local copies, waits for them, and re-layouts  1.67 us (2%)
    pallas_call x1, Pallas kernels, per_device(): pl.pallas_call(kernel, out_shape=jax.ShapeDtypeStruct((ROWS, OWN), F32),...  69.1 us
    unnamed x1, local copies, waits for them, and re-layouts  1.67 us

profile of v6, /device:TPU:1, one launch (start us, length us, event | category | flops | bytes accessed | tf_op | source)
XLA Modules:
  0.0 70.7 jit_solution(6205803942884675509)
XLA Ops:
  0.0 69.1 %filter_and_orthonormalize.1 = f32[32,2048]{1,0:T(8,128)} custom-call(f32[32,2048]{1,0:T(8,128)} %orbitals_hbm.1, s32[8,512]{1,0:T(8,128)} %connectivity_hbm.1, s32[1,256]{1,0:T(1,128)} %bitcast.2, s32[1,256]{1,0:T(1,128)} %bitcast.3, bf16[8,512,512]{2,1,0:T(8,128)(2,1)} %matrices_hbm.1), custom_call_target="tpu_custom_call" | custom-call | tf_op jit(solution)/shard_map/filter_and_orthonormalize/pallas_call | solution.py:585
  69.1 1.7 %copy.7 = f32[32,2048]{1,0:T(8,128)} copy(f32[32,2048]{1,0:T(8,128)} %filter_and_orthonormalize.1) | data formatting | bytes 524288
